TPU v7x, 128 devices: a whole 4x4x4 slice. The times are simulated.
128 devices in a mesh: tab: 32 (over x, y, core), rep: 4 (over z).
Axes of the slice: x: 4, y: 4, z: 4, core: 2. Of those that a mesh axis runs over, the one named last changes fastest.
Arguments:
- pooled: bfloat16 [64, 16384, 128], P('tab', 'rep'), may hold values from -6 to 6
- widths: int32 [64], replicated, may hold values from 16 to 128, as said below
- placement: int32 [64], replicated, may hold values from 0 to 63, each once
- route: int32 [4, 4096], P('rep'), may hold values from 0 to 4095, each once within a row
- labels: int32 [4, 4096], P('rep'), may hold values 0 or 1
- proj: bfloat16 [64, 128, 32], replicated, may hold values from -0.5 to 0.5
- senet_in: float32 [64, 32], replicated, may hold values from -6 to 6
- senet_out: float32 [32, 64], replicated, may hold values from -1 to 1
- bilinear: float32 [32, 32], replicated, may hold values from -1 to 1
- w_first: bfloat16 [4096, 256], replicated, may hold values from -0.09375 to 0.09375
- w_second: bfloat16 [256, 256], replicated, may hold values from -0.75 to 0.75
- w_last: bfloat16 [256], replicated, may hold values from -0.375 to 0.375
Outputs:
- scores: float32 [4, 4096], P('rep', 'tab')
- d_pooled: bfloat16 [64, 16384, 128], P('tab', 'rep')
- d_proj: float32 [64, 128, 32], P('tab')
- d_senet_in: float32 [64, 32], replicated
- d_senet_out: float32 [32, 64], replicated
- d_bilinear: float32 [32, 32], replicated
- d_first: float32 [4096, 256], P('tab')
- d_second: float32 [256, 256], replicated
- d_last: float32 [256], replicated
Inputs may be any that keep to these rules, and one draw needn't show every extreme that they name: `widths`: each field's width is 128, 64, 32 or 16. `placement`: a permutation of the fields. `route`: each row is a permutation of 0 to 4095.
All inputs are finite; a program needn't handle non-finite values. No bound on the sum of `labels` on one device may be relied on, other than what follows from the above.
Results may differ from a plain program's by a relative error of at most 0.017.
Values may be sent and summed in bfloat16 or wider, within the bound.
A program may use at most 64 MiB of HBM per device.

v0:
```python
import jax
import jax.numpy as jnp
from jax import lax
from jax.sharding import PartitionSpec as P


def sent_to_all(value, axis):
    peers = lax.axis_size(axis)
    return lax.all_to_all(
        jnp.broadcast_to(value[None], (peers, *value.shape)), axis, 0, 0, tiled=True
    )


def of_everyone(value, axis):
    everything = sent_to_all(value, axis)
    return jnp.sum(everything.astype(jnp.float32), axis=0)


def laid_out(pieces, dim):
    lengths = list(pieces.shape[1:])
    lengths[dim] *= pieces.shape[0]
    return jnp.moveaxis(pieces, 0, dim).reshape(lengths)


def collect(value, axis, dim):
    pieces = sent_to_all(value, axis)
    return laid_out(pieces, dim)


def silu_slope(pre_act):
    logistic = jax.nn.sigmoid(pre_act)
    return logistic * (1.0 + pre_act * (1.0 - logistic))


def bilinear_forward(fields_in, bilinear, factor):
    product = jnp.einsum("fnc,cd->fnd", fields_in, bilinear)
    others = jnp.sum(fields_in, axis=0, keepdims=True) - fields_in
    return (product * others * factor, product, others)


def bilinear_backward(fields_in, product, others, upstream, bilinear, factor):
    d_product = upstream * others * factor
    d_others = upstream * product * factor
    d_fields = jnp.einsum("fnd,cd->fnc", d_product, bilinear)
    d_fields = d_fields + jnp.sum(d_others, axis=0, keepdims=True) - d_others
    d_weight = jnp.einsum("fnc,fnd->cd", fields_in, d_product)
    return (d_fields, d_weight)


def owner_pass(embeds, targets, senet_in, senet_out, bilinear, w_first, w_second, w_last):
    count = embeds.shape[0]
    width = embeds.shape[2]
    hidden = w_second.shape[0]
    factor = count ** (-0.5)
    first = w_first.reshape(2, count, width, hidden)
    dense = embeds.astype(jnp.float32)
    squeeze = jnp.mean(dense, axis=2)
    pre_one = jnp.einsum("fn,fr->rn", squeeze, senet_in)
    act_one = jax.nn.silu(pre_one)
    pre_two = jnp.einsum("rn,rf->fn", act_one, senet_out)
    weights = jax.nn.sigmoid(pre_two)
    scaled = weights[:, :, None] * dense
    plain_out, plain_prod, plain_rest = bilinear_forward(dense, bilinear, factor)
    scaled_out, scaled_prod, scaled_rest = bilinear_forward(scaled, bilinear, factor)
    joined = jnp.stack([plain_out, scaled_out]).astype(jnp.bfloat16)
    pre_hidden = jnp.einsum("kfnc,kfch->nh", joined, first, preferred_element_type=jnp.float32)
    hidden_one = jax.nn.silu(pre_hidden).astype(jnp.bfloat16)
    pre_second = jnp.dot(hidden_one, w_second, preferred_element_type=jnp.float32)
    hidden_two = jax.nn.silu(pre_second).astype(jnp.bfloat16)
    logits = jnp.dot(hidden_two, w_last, preferred_element_type=jnp.float32)
    grad_logit = jax.nn.sigmoid(logits) - targets
    d_last = jnp.dot(grad_logit, hidden_two.astype(jnp.float32))
    last_wide = w_last.astype(jnp.float32)
    d_pre_two = (grad_logit[:, None] * last_wide[None, :] * silu_slope(pre_second)).astype(
        jnp.bfloat16
    )
    d_second = jnp.dot(hidden_one.T, d_pre_two, preferred_element_type=jnp.float32)
    back_two = jnp.dot(d_pre_two, w_second.T, preferred_element_type=jnp.float32)
    d_pre_one = (back_two * silu_slope(pre_hidden)).astype(jnp.bfloat16)
    d_first = jnp.einsum(
        "kfnc,nh->kfch", joined, d_pre_one, preferred_element_type=jnp.float32
    ).reshape(-1, hidden)
    d_joined = jnp.einsum("nh,kfch->kfnc", d_pre_one, first, preferred_element_type=jnp.float32)
    d_plain, d_bil_plain = bilinear_backward(
        dense, plain_prod, plain_rest, d_joined[0], bilinear, factor
    )
    d_scaled, d_bil_scaled = bilinear_backward(
        scaled, scaled_prod, scaled_rest, d_joined[1], bilinear, factor
    )
    d_weights = jnp.sum(d_scaled * dense, axis=2)
    d_pre_w = d_weights * weights * (1.0 - weights)
    d_senet_out = jnp.einsum("rn,fn->rf", act_one, d_pre_w)
    d_act = jnp.einsum("fn,rf->rn", d_pre_w, senet_out) * silu_slope(pre_one)
    d_senet_in = jnp.einsum("fn,rn->fr", squeeze, d_act)
    d_squeeze = jnp.einsum("rn,fr->fn", d_act, senet_in)
    d_embeds = d_plain + weights[:, :, None] * d_scaled + d_squeeze[:, :, None] / width
    small = (d_senet_in, d_senet_out, d_bil_plain + d_bil_scaled, d_second, d_last)
    return (logits, d_embeds.astype(jnp.bfloat16), small, d_first, joined, d_pre_one)


def shards(
    pooled,
    widths,
    placement,
    route,
    labels,
    proj,
    senet_in,
    senet_out,
    bilinear,
    w_first,
    w_second,
    w_last,
):
    tab_count = lax.axis_size("tab")
    tab_index = lax.axis_index("tab")
    local_count = pooled.shape[0]
    rep_rows = pooled.shape[1]
    padded = pooled.shape[2]
    field_count = placement.shape[0]
    owner_rows = rep_rows // tab_count
    field_ids = jnp.arange(field_count, dtype=jnp.int32)
    matches = placement[:, None] == field_ids[None, :]
    slot_width = jnp.sum(jnp.where(matches, widths[None, :], 0), axis=1)
    slot_mask = (jnp.arange(padded, dtype=jnp.int32)[None, :] < slot_width[:, None]).astype(
        jnp.bfloat16
    )
    inverse = jnp.zeros_like(placement).at[placement].set(field_ids)
    targets = lax.dynamic_slice_in_dim(labels[0], tab_index * owner_rows, owner_rows).astype(
        jnp.float32
    )
    first_slot = tab_index * local_count
    local_fields = lax.dynamic_slice_in_dim(placement, first_slot, local_count)
    local_mask = lax.dynamic_slice_in_dim(slot_mask, first_slot, local_count, 0)
    local_proj = jnp.take(proj, local_fields, axis=0)
    masked = pooled * local_mask[:, None, :]
    embed_local = jnp.einsum(
        "fnc,fcd->fnd", masked, local_proj, preferred_element_type=jnp.float32
    ).astype(jnp.bfloat16)
    embed_slot = lax.all_to_all(embed_local, "tab", split_axis=1, concat_axis=0, tiled=True)
    logits, d_embeds, small, d_first_part, joined, d_pre_one = owner_pass(
        embed_slot[inverse], targets, senet_in, senet_out, bilinear, w_first, w_second, w_last
    )
    d_slot = d_embeds[placement]
    d_local = lax.all_to_all(d_slot, "tab", split_axis=0, concat_axis=1, tiled=True)
    back = jnp.einsum("fnd,fcd->fnc", d_local, local_proj, preferred_element_type=jnp.float32)
    back = (back * local_mask[:, None, :]).astype(jnp.bfloat16)
    d_proj_part = jnp.einsum("fnc,fnd->fcd", masked, d_local, preferred_element_type=jnp.float32)
    d_proj = of_everyone(d_proj_part.astype(jnp.bfloat16), "rep").astype(jnp.float32)
    first_tab = lax.psum_scatter(
        d_first_part.astype(jnp.bfloat16), "tab", scatter_dimension=0, tiled=True
    )
    d_first = of_everyone(first_tab, "rep").astype(jnp.float32)
    part_in, part_out, part_bil, part_second, part_last = small
    d_senet_in, d_senet_out, d_bilinear, d_second, d_last = lax.psum(
        (part_in, part_out, part_bil, part_second, part_last), ("tab", "rep")
    )
    all_logits = collect(logits, "tab", 0)
    wanted = lax.dynamic_slice_in_dim(route[0], tab_index * owner_rows, owner_rows)
    scores = jnp.take(all_logits, wanted)[None, :]
    return (scores, back, d_proj, d_senet_in, d_senet_out, d_bilinear, d_first, d_second, d_last)


def solution(mesh):
    placed = (
        P("tab", "rep", None),
        P(),
        P(),
        P("rep", None),
        P("rep", None),
        P(),
        P(),
        P(),
        P(),
        P(),
        P(),
        P(),
    )
    return jax.shard_map(
        shards,
        mesh=mesh,
        in_specs=placed,
        out_specs=(
            P("rep", "tab"),
            P("tab", "rep", None),
            P("tab", None, None),
            P(),
            P(),
            P(),
            P("tab", None),
            P(),
            P(),
        ),
        check_vma=False,
    )
```

profile of v0, /device:TPU:0, one launch (start us, length us, event | category | flops | bytes accessed | tf_op | source)
XLA Modules:
  0.0 224.7 jit_solution(7572727441180644628)
XLA Ops:
  9.9 1.6 gather_fusion
  11.5 2.4 %convolution_convert_fusion = bf16[2,4096,32]{1,2,0:T(8,128)(2,1)S(1)} fusion(bf16[2,4096,128]{2,1,0:T(8,128)(2,1)} %param.12, bf16[2,128]{1,0:T(2,128)(2,1)S(1)} %get-tuple-element.22, bf16[2,128,32]{1,2,0:T(8,128)(2,1)S(1)} %gather_fusion, pred[2]{0:T(512)(128)(4,1)S(1)} %get-tuple-element.17), kind=kOutput, calls=%fused_computation.7 | convolution fusion | flops 68427776 | bytes 2638338 | tf_op jit(solution)/shard_map/fnc,fcd->fnd/dot_general | solution.py:137
  14.0 3.8 %copy.56 = bf16[2,4096,32]{2,0,1:T(2,128)(2,1)} copy(bf16[2,4096,32]{1,2,0:T(8,128)(2,1)S(1)} %convolution_convert_fusion) | data formatting | bytes 1048576 | tf_op jit(solution)/shard_map/convert_element_type | solution.py:139
  17.8 5.9 %reshape.152 = bf16[32,2,4096]{2,1,0:T(2,128)(2,1)} reshape(bf16[4096,2,32]{2,1,0:T(2,128)(2,1)} %bitcast.166) | data formatting | bytes 1048576
  23.7 7.4 %all-to-all-start = ((bf16[32,2,4096]{2,1,0:T(2,128)(2,1)}), bf16[32,2,4096]{2,1,0:T(2,128)(2,1)S(1)}, u32[]{:S(2)}, u32[]{:S(2)}) async-start(bf16[32,2,4096]{2,1,0:T(2,128)(2,1)} %reshape.152), calls=%async_computation | async-start | bytes 1048576 | tf_op jit(solution)/shard_map/all_to_all | solution.py:140
  32.0 10.2 %all-to-all-done = bf16[32,2,4096]{2,1,0:T(2,128)(2,1)S(1)} async-done(((bf16[32,2,4096]{2,1,0:T(2,128)(2,1)}), bf16[32,2,4096]{2,1,0:T(2,128)(2,1)S(1)}, u32[]{:S(2)}, u32[]{:S(2)}) %all-to-all-start) | async-done | bytes 524320 | tf_op jit(solution)/shard_map/all_to_all | solution.py:140
  42.2 2.0 reshape.153
  44.2 4.7 %copy.73 = bf16[2,32,128,32]{2,3,0,1:T(8,128)(2,1)S(1)} copy(bf16[2,32,128,32]{3,0,2,1:T(2,128)(2,1)} %bitcast.167) | data formatting | bytes 1048576 | tf_op jit(solution)/shard_map/all_to_all | solution.py:140
  53.7 2.1 convolution_convert_fusion.1
  57.1 4.1 %all-to-all-start.1 = ((f32[32,1,128]{2,1,0:T(1,128)}), f32[32,1,128]{2,1,0:T(1,128)S(1)}, u32[]{:S(2)}, u32[]{:S(2)}) async-start(f32[32,1,128]{2,1,0:T(1,128)} %broadcast_in_dim.45), calls=%async_computation.1 | async-start | bytes 32768 | tf_op jit(solution)/shard_map/all_to_all | solution.py:9
  62.3 1.7 copy-done.3
  67.9 2.7 %fusion.14 = bf16[64,128,32]{1,2,0:T(8,128)(2,1)S(1)} fusion(f32[64,128,32]{1,2,0:T(8,128)} %get-tuple-element.28, bf16[64,128,32]{1,2,0:T(8,128)(2,1)S(1)} %gather_fusion.1, f32[2,64,128,32]{2,3,1,0:T(8,128)} %copy-done.1, f32[64,128]{1,0:T(8,128)S(1)} %fusion.24, f32[128,32]{0,1:T(8,128)S(1)} %get-tuple-element.9, f32[64,128]{1,0:T(8,128)S(1)} %fusion.28, ...), kind=kOutput, calls=%fused_computation.30 | convolution fusion | flops 19922944 | bytes 5345280 | tf_op jit(solution)/shard_map/fnd,cd->fnc/dot_general | solution.py:44
  72.1 7.4 %all-to-all-start.2 = ((bf16[64,128,32]{1,2,0:T(8,128)(2,1)}), bf16[64,128,32]{1,2,0:T(8,128)(2,1)S(1)}, u32[]{:S(2)}, u32[]{:S(2)}) async-start(bf16[64,128,32]{1,2,0:T(8,128)(2,1)} %gather_fusion.3), calls=%async_computation.2 | async-start | bytes 1048576 | tf_op jit(solution)/shard_map/all_to_all | solution.py:145
  79.6 1.6 fusion.34
  81.3 69.8 %all-reduce = (f32[64,32]{0,1:T(8,128)}, f32[32,64]{1,0:T(8,128)}, f32[32,32]{1,0:T(8,128)}, f32[256]{0:T(256)}) all-reduce(f32[64,32]{0,1:T(8,128)S(1)} %fusion.68, f32[32,64]{1,0:T(8,128)S(1)} %fusion.79, f32[32,32]{1,0:T(8,128)S(1)} %fusion.34, f32[256]{0:T(256)S(1)} %bitcast.171), channel_id=1, replica_groups=mesh['tab'=32,'rep'=4] {'tab','rep'}, use_global_device_ids=true, to_apply=%region_9.10 | all-reduce | flops 5376 | bytes 43008 | tf_op jit(solution)/shard_map/psum | solution.py:155
  152.2 2.2 fusion.29
  155.1 3.3 %all-to-all-start.3 = ((bf16[4,2,128,32]{2,3,1,0:T(8,128)(2,1)}), bf16[4,2,128,32]{2,3,1,0:T(8,128)(2,1)S(1)}, u32[]{:S(2)}, u32[]{:S(2)}) async-start(bf16[4,2,128,32]{2,3,1,0:T(8,128)(2,1)} %broadcast_in_dim.49), calls=%async_computation.3 | async-start | bytes 131072 | tf_op jit(solution)/shard_map/all_to_all | solution.py:9
  159.5 4.4 %all-to-all-done.3 = bf16[4,2,128,32]{2,3,1,0:T(8,128)(2,1)S(1)} async-done(((bf16[4,2,128,32]{2,3,1,0:T(8,128)(2,1)}), bf16[4,2,128,32]{2,3,1,0:T(8,128)(2,1)S(1)}, u32[]{:S(2)}, u32[]{:S(2)}) %all-to-all-start.3) | async-done | bytes 65568 | tf_op jit(solution)/shard_map/all_to_all | solution.py:9
  164.0 1.6 broadcast_in_dim.82
  165.5 3.4 %all-to-all-start.4 = ((bf16[4,128,256]{2,1,0:T(8,128)(2,1)}), bf16[4,128,256]{2,1,0:T(8,128)(2,1)S(1)}, u32[]{:S(2)}, u32[]{:S(2)}) async-start(bf16[4,128,256]{2,1,0:T(8,128)(2,1)} %broadcast_in_dim.82), calls=%async_computation.5 | async-start | bytes 524288 | tf_op jit(solution)/shard_map/all_to_all | solution.py:9
  168.9 2.3 %fusion = bf16[2,4096,128]{2,1,0:T(8,128)(2,1)} fusion(f32[2,128]{1,0:T(2,128)S(1)} %get-tuple-element.21, bf16[32,2,4,8,128]{4,3,2,1,0:T(8,128)(2,1)S(1)} %bitcast.170, bf16[2,128,32]{1,2,0:T(8,128)(2,1)S(1)} %gather_fusion, pred[2]{0:T(512)(128)(4,1)S(1)} %get-tuple-element.17), kind=kOutput, calls=%fused_computation.6 | convolution fusion | flops 69214208 | bytes 2638850 | tf_op jit(solution)/shard_map/fnd,fcd->fnc/dot_general | solution.py:146
  171.8 3.8 %all-to-all-done.4 = bf16[4,128,256]{2,1,0:T(8,128)(2,1)S(1)} async-done(((bf16[4,128,256]{2,1,0:T(8,128)(2,1)}), bf16[4,128,256]{2,1,0:T(8,128)(2,1)S(1)}, u32[]{:S(2)}, u32[]{:S(2)}) %all-to-all-start.4) | async-done | bytes 262176 | tf_op jit(solution)/shard_map/all_to_all | solution.py:9
  176.3 39.3 %all-reduce.3.cloned.1.call-done = f32[256,256]{1,0:T(8,128)} async-done(((f32[256,256]{1,0:T(8,128)}), f32[256,256]{1,0:T(8,128)}) %all-reduce.3.cloned.1.call-update) | async-done | bytes 262160 | tf_op jit(solution)/shard_map/psum | solution.py:155
  215.6 1.7 copy.92
  (74 shorter events, 19.6 us)
Async XLA Ops:
  8.0 43.5 %copy-start = (bf16[4096,256]{1,0:T(8,128)(2,1)S(1)}, bf16[4096,256]{1,0:T(8,128)(2,1)}, u32[]{:S(2)}) copy-start(bf16[4096,256]{1,0:T(8,128)(2,1)} %param.21) | copy-start | bytes 6291460
  17.8 13.4 %copy-start.11 = (bf16[256]{0:T(256)(128)(2,1)S(1)}, bf16[256]{0:T(256)(128)(2,1)}, u32[]{:S(2)}) copy-start(bf16[256]{0:T(256)(128)(2,1)} %param.23) | copy-start | bytes 1540
  17.8 13.4 %copy-start.8 = (s32[64]{0:T(128)S(1)}, s32[64]{0:T(128)}, u32[]{:S(2)}) copy-start(s32[64]{0:T(128)} %param.14) | copy-start | bytes 772
  23.7 18.5 %all-to-all-start = ((bf16[32,2,4096]{2,1,0:T(2,128)(2,1)}), bf16[32,2,4096]{2,1,0:T(2,128)(2,1)S(1)}, u32[]{:S(2)}, u32[]{:S(2)}) async-start(bf16[32,2,4096]{2,1,0:T(2,128)(2,1)} %reshape.152), calls=%async_computation | async-start | bytes 1048576 | tf_op jit(solution)/shard_map/all_to_all | solution.py:140
  31.1 132.8 %reduce-scatter.2.cloned.1.call-start = ((), (), s32[]{:S(2)}) async-start(), calls=%async_computation.6 | async-start | bytes 2162688 | tf_op jit(solution)/shard_map/reduce_scatter | solution.py:150
  48.8 0.8 copy-start.7
  48.9 1.0 copy-start.10
  48.9 1.3 copy-start.6
  50.6 1.0 copy-start.4
  50.9 1.2 copy-start.2
  51.6 0.9 copy-start.9
  57.1 15.0 %all-to-all-start.1 = ((f32[32,1,128]{2,1,0:T(1,128)}), f32[32,1,128]{2,1,0:T(1,128)S(1)}, u32[]{:S(2)}, u32[]{:S(2)}) async-start(f32[32,1,128]{2,1,0:T(1,128)} %broadcast_in_dim.45), calls=%async_computation.1 | async-start | bytes 32768 | tf_op jit(solution)/shard_map/all_to_all | solution.py:9
  61.2 154.3 %all-reduce.3.cloned.1.call-start = ((), (), s32[]{:S(2)}) async-start(), calls=%async_computation.7 | async-start | bytes 524288 | tf_op jit(solution)/shard_map/psum | solution.py:155
  62.0 2.8 %copy-start.1 = (f32[2,64,128,32]{2,3,1,0:T(8,128)}, f32[2,64,128,32]{2,3,1,0:T(8,128)S(1)}, u32[]{:S(2)}) copy-start(f32[2,64,128,32]{2,3,1,0:T(8,128)S(1)} %convolution_bitcast_fusion) | copy-start | bytes 6291460
  62.0 2.0 copy-start.3
  62.0 2.3 %copy-start.5 = (f32[64,128,32]{1,2,0:T(8,128)S(1)}, f32[64,128,32]{1,2,0:T(8,128)}, u32[]{:S(2)}) copy-start(f32[64,128,32]{1,2,0:T(8,128)} %copy-done.4) | copy-start | bytes 3145732
  72.1 80.2 %all-to-all-start.2 = ((bf16[64,128,32]{1,2,0:T(8,128)(2,1)}), bf16[64,128,32]{1,2,0:T(8,128)(2,1)S(1)}, u32[]{:S(2)}, u32[]{:S(2)}) async-start(bf16[64,128,32]{1,2,0:T(8,128)(2,1)} %gather_fusion.3), calls=%async_computation.2 | async-start | bytes 1048576 | tf_op jit(solution)/shard_map/all_to_all | solution.py:145
  155.1 8.9 %all-to-all-start.3 = ((bf16[4,2,128,32]{2,3,1,0:T(8,128)(2,1)}), bf16[4,2,128,32]{2,3,1,0:T(8,128)(2,1)S(1)}, u32[]{:S(2)}, u32[]{:S(2)}) async-start(bf16[4,2,128,32]{2,3,1,0:T(8,128)(2,1)} %broadcast_in_dim.49), calls=%async_computation.3 | async-start | bytes 131072 | tf_op jit(solution)/shard_map/all_to_all | solution.py:9
  165.5 10.1 %all-to-all-start.4 = ((bf16[4,128,256]{2,1,0:T(8,128)(2,1)}), bf16[4,128,256]{2,1,0:T(8,128)(2,1)S(1)}, u32[]{:S(2)}, u32[]{:S(2)}) async-start(bf16[4,128,256]{2,1,0:T(8,128)(2,1)} %broadcast_in_dim.82), calls=%async_computation.5 | async-start | bytes 524288 | tf_op jit(solution)/shard_map/all_to_all | solution.py:9
Sparse Core Ops, SparseCore 0:
  55.9 78.0 reduce-scatter.1
Sparse Core Ops, SparseCore 1:
  68.0 147.5 all-reduce.2
where the time goes:
time: 226 us; the launch traced here: 225 us
  blocking collectives  69.8 us (31%)
  waiting for transfers between devices  57.7 us (26%)
  local copies, waits for them, and re-layouts  29.1 us (13%)
  starting transfers between devices  25.7 us (11%)
  matrix products  20.3 us (9%)
  between operations  15.8 us (7%)
  other arithmetic  6.22 us (3%)
    psum x1, blocking collectives, shards(): lax.psum((part_in, part_out, part_bil, part_second, part_last), ('tab', '...  69.8 us
    psum x1, waiting for transfers between devices, shards(): lax.psum((part_in, part_out, part_bil, part_second, part_last), ('tab', '...  39.3 us
    unnamed x28, local copies, waits for them, and re-layouts  12.2 us
    all_to_all x3, starting transfers between devices, sent_to_all(): lax.all_to_all(jnp.broadcast_to(value[None], (peers, *value.shape)), axis...  10.8 us
    all_to_all x1, waiting for transfers between devices, shards(): lax.all_to_all(embed_local, 'tab', split_axis=1, concat_axis=0, tiled=True)  10.2 us
    all_to_all x3, waiting for transfers between devices, sent_to_all(): lax.all_to_all(jnp.broadcast_to(value[None], (peers, *value.shape)), axis...  8.18 us
    all_to_all x1, starting transfers between devices, shards(): lax.all_to_all(embed_local, 'tab', split_axis=1, concat_axis=0, tiled=True)  7.43 us
    all_to_all x1, starting transfers between devices, shards(): lax.all_to_all(d_slot, 'tab', split_axis=0, concat_axis=1, tiled=True)  7.38 us
  transfers between devices with their start and end apart: 7, of which 4 were waited for; matrix products, arithmetic and copies ran while one was open for 10% of the time, Pallas kernels for 0%

commit v1 on v0

v1 whole, which is shorter than its diff:
```python
import functools

import jax
import jax.numpy as jnp
from jax import lax
from jax.experimental import pallas as pl
from jax.experimental.pallas import tpu as pltpu
from jax.sharding import PartitionSpec as P

F32 = jnp.float32
BF = jnp.bfloat16
HI = lax.Precision.HIGHEST
NN = (((1,), (0,)), ((), ()))
NT = (((1,), (1,)), ((), ()))
TN = (((0,), (0,)), ((), ()))

FIELDS = 64
E = 32
TAB = 32
REP = 4
SIDE = 4
LANES = 128
HID = 256
BLOCK = 272
SMALL = 144
FACTOR = 0.125


def mm(a, b, dims, precision=None):
    return lax.dot_general(a, b, dims, precision=precision, preferred_element_type=F32)


def slope(u):
    s = jax.nn.sigmoid(u)
    return s * (1.0 + u * (1.0 - s))


def iota(shape, dim):
    return lax.broadcasted_iota(jnp.int32, shape, dim)


def project_kernel(tab_ref, place_ref, width_ref, pooled_ref, proj_ref, e_ref, pt_ref, mask_ref, inv_ref):
    i = pl.program_id(0)
    j = pl.program_id(1)
    field = place_ref[2 * tab_ref[0] + i]
    width = width_ref[field]

    @pl.when((i == 0) & (j == 0))
    def _():
        def put(s, _):
            inv_ref[place_ref[s]] = s
            return 0

        lax.fori_loop(0, FIELDS, put, 0)

    eye = (iota((E, E), 0) == iota((E, E), 1)).astype(BF)
    keep = iota((E, LANES), 1) < width
    turned = jnp.where(keep, mm(eye, proj_ref[0], NT), 0.0).astype(BF)
    pt_ref[...] = turned
    mask_ref[...] = keep.astype(F32)
    out = mm(turned, pooled_ref[0], NT).astype(BF)
    for d in range(out.shape[1] // LANES):
        e_ref[d, 0] = out[:, d * LANES : (d + 1) * LANES]


def project(tab, placement, widths, pooled, proj):
    rows = pooled.shape[1]
    steps = 2
    chunk = rows // steps
    grid_spec = pltpu.PrefetchScalarGridSpec(
        num_scalar_prefetch=3,
        grid=(2, steps),
        in_specs=[
            pl.BlockSpec((1, chunk, LANES), lambda i, j, t, p, w: (i, j, 0)),
            pl.BlockSpec((1, LANES, E), lambda i, j, t, p, w: (p[2 * t[0] + i], 0, 0)),
        ],
        out_specs=[
            pl.BlockSpec((chunk // LANES, 1, E, LANES), lambda i, j, t, p, w: (j, i, 0, 0)),
            pl.BlockSpec((E, LANES), lambda i, j, t, p, w: (i, 0)),
            pl.BlockSpec((E, LANES), lambda i, j, t, p, w: (i, 0)),
            pl.BlockSpec(memory_space=pltpu.SMEM),
        ],
    )
    return pl.pallas_call(
        project_kernel,
        grid_spec=grid_spec,
        out_shape=[
            jax.ShapeDtypeStruct((TAB, 2, E, LANES), BF),
            jax.ShapeDtypeStruct((2 * E, LANES), BF),
            jax.ShapeDtypeStruct((2 * E, LANES), F32),
            jax.ShapeDtypeStruct((FIELDS,), jnp.int32),
        ],
        compiler_params=pltpu.CompilerParams(vmem_limit_bytes=16 << 20),
        name="project",
    )(tab, placement, widths, pooled, proj)


def send(src, dst, ssem, rsem, dev):
    pltpu.make_async_remote_copy(
        src_ref=src, dst_ref=dst, send_sem=ssem, recv_sem=rsem, device_id=dev,
        device_id_type=pl.DeviceIdType.MESH,
    ).start()


def got(dst, ssem, rsem, dev):
    pltpu.make_async_remote_copy(
        src_ref=dst, dst_ref=dst, send_sem=ssem, recv_sem=rsem, device_id=dev,
        device_id_type=pl.DeviceIdType.MESH,
    ).wait_recv()


def sent(src, ssem, rsem, dev):
    pltpu.make_async_remote_copy(
        src_ref=src, dst_ref=src, send_sem=ssem, recv_sem=rsem, device_id=dev,
        device_id_type=pl.DeviceIdType.MESH,
    ).wait_send()


def main_kernel(
    inv_ref, place_ref, e_ref, labels_ref, sin_ref, sout_ref, bil_ref, w2_ref, wl_ref, w1_hbm, pooled_hbm,
    rd_ref, lg_ref, df_ref, ag_ref, smf_ref, dpt_ref,
    w1, xs, recv, emb, prod, du, sq, wts, dpw, dsq, js, jp, dpb, d2, d2p, dbil, demb, dslot, dfb, r1, r2, rz, sr, dz,
    load_sem, es, er, ds, dr, ls, lr, gs, gr, ps, pr, s1, q1, s2, q2, sz, qz, ss, sq_r, sd, qd,
):
    t = lax.axis_index("tab")
    r = lax.axis_index("rep")
    c = lax.rem(t, 2)
    n = t // 2
    x = n // SIDE
    y = lax.rem(n, SIDE)
    a = x + c * (y - x)
    b = y + c * (x - y)

    def at(a_, b_):
        return ((a_ + c * (b_ - a_)) * SIDE + (b_ + c * (a_ - b_))) * 2 + c

    def block_of(tab):
        c_ = lax.rem(tab, 2)
        n_ = tab // 2
        x_ = n_ // SIDE
        y_ = lax.rem(n_, SIDE)
        return 16 * c_ + SIDE * (x_ + c_ * (y_ - x_)) + y_ + c_ * (x_ - y_)

    mate = {"tab": t + 1 - 2 * c}
    barrier = pltpu.get_barrier_semaphore()

    def hello(i, _):
        pl.semaphore_signal(barrier, inc=1, device_id={"tab": lax.rem(t + i, TAB)}, device_id_type=pl.DeviceIdType.MESH)
        return 0

    lax.fori_loop(1, TAB, hello, 0)
    for d in range(1, REP):
        pl.semaphore_signal(barrier, inc=1, device_id={"rep": lax.rem(r + d, REP)}, device_id_type=pl.DeviceIdType.MESH)

    load_w1 = pltpu.make_async_copy(w1_hbm, w1, load_sem.at[0])
    load_x = pltpu.make_async_copy(pooled_hbm, xs, load_sem.at[1])
    load_w1.start()
    load_x.start()

    small_rows = (lax.rem(iota((HID, E), 0), E) == iota((HID, E), 1)).astype(BF)
    small_cols = (lax.rem(iota((E, HID), 1), E) == iota((E, HID), 0)).astype(BF)
    diag = (iota((HID, HID), 0) // E) == (iota((HID, HID), 1) // E)
    bil = bil_ref[...].astype(BF)
    tall = mm(small_rows, bil, NN).astype(BF)
    tall_t = mm(small_rows, bil, NT).astype(BF)
    kron = jnp.where(diag, mm(tall, small_cols, NN), 0.0).astype(BF)
    kron_t = jnp.where(diag, mm(tall_t, small_cols, NN), 0.0).astype(BF)
    square = iota((LANES, LANES), 0) == iota((LANES, LANES), 1)
    label_row = labels_ref[:, pl.ds(pl.multiple_of(t * LANES, LANES), LANES)].astype(F32)
    target = jnp.sum(jnp.where(square, label_row, 0.0), axis=1, keepdims=True)

    pl.semaphore_wait(barrier, TAB - 1 + REP - 1)

    def pair(p):
        return pl.ds(p * 2, 2)

    def e_send(i, _):
        p = lax.rem(t + i, TAB)
        send(e_ref.at[p], recv.at[pair(t)], es.at[p], er.at[t], {"tab": p})
        return 0

    lax.fori_loop(1, TAB, e_send, 0)
    recv[pair(t)] = e_ref[t]

    def e_wait(i, _):
        p = lax.rem(t + i, TAB)
        got(recv.at[pair(p)], es.at[p], er.at[p], {"tab": p})
        return 0

    lax.fori_loop(1, TAB, e_wait, 0)

    def rows32(f):
        return pl.ds(pl.multiple_of(f * E, E), E)

    def by_field(f, _):
        emb[rows32(f), :] = recv[inv_ref[f]]
        return 0

    lax.fori_loop(0, FIELDS, by_field, 0)

    groups = FIELDS // 8

    def rows256(g):
        return pl.ds(pl.multiple_of(g * HID, HID), HID)

    def rows8(g):
        return pl.ds(pl.multiple_of(g * 8, 8), 8)

    def cube(v):
        return v.reshape(8, E, LANES)

    def flat(v):
        return v.reshape(HID, LANES)

    def first_pass(g, total):
        u = cube(emb[rows256(g), :].astype(F32))
        sq[rows8(g), :] = jnp.sum(u, axis=1) * (1.0 / E)
        return total + jnp.sum(u, axis=0)

    zero = jnp.zeros((E, LANES), F32)
    total = lax.fori_loop(0, groups, first_pass, zero)
    squeeze = sq[...]
    pre_one = mm(sin_ref[...], squeeze, TN, HI)
    act_one = pre_one * jax.nn.sigmoid(pre_one)
    weights = jax.nn.sigmoid(mm(sout_ref[...], act_one, TN, HI))
    wts[...] = weights

    def scaled_of(g):
        u = cube(emb[rows256(g), :].astype(F32))
        return u, u * wts[rows8(g), :][:, None, :]

    def second_pass(g, tot):
        return tot + jnp.sum(scaled_of(g)[1], axis=0)

    total_s = lax.fori_loop(0, groups, second_pass, zero)

    load_w1.wait()

    def third_pass(g, acc):
        u, sc = scaled_of(g)
        for k, (v, vb, tot) in enumerate(((u, emb[rows256(g), :], total), (sc, flat(sc).astype(BF), total_s))):
            p = mm(kron_t, vb, NN)
            prod[k, rows256(g), :] = p
            j = flat(cube(p) * (tot[None] - v) * FACTOR).astype(BF)
            chip = k * groups + g
            js[chip] = j[:LANES]
            js[16 + lax.rem(chip, SIDE) * SIDE + chip // SIDE] = j[LANES:]
            acc = acc + mm(j, w1[rows256(k * groups + g), :], TN)
        return acc

    pre_hidden = lax.fori_loop(0, groups, third_pass, jnp.zeros((LANES, HID), F32))
    half = pl.ds((1 - c) * 16, 16)
    send(js.at[half], jp, ps.at[0], pr.at[0], mate)

    h1 = (pre_hidden * jax.nn.sigmoid(pre_hidden)).astype(BF)
    pre_second = mm(h1, w2_ref[...], NN)
    h2 = (pre_second * jax.nn.sigmoid(pre_second)).astype(BF).astype(F32)
    wl = wl_ref[...].astype(F32)
    logit = jnp.sum(h2 * wl, axis=1, keepdims=True)
    lg_ref[t] = jnp.sum(jnp.where(square, logit, 0.0), axis=0, keepdims=True)

    def l_send(i, _):
        p = lax.rem(t + i, TAB)
        send(lg_ref.at[t], lg_ref.at[t], ls.at[p], lr.at[t], {"tab": p})
        return 0

    lax.fori_loop(1, TAB, l_send, 0)
    grad = jax.nn.sigmoid(logit) - target
    d_last = jnp.sum(grad * h2, axis=0, keepdims=True)
    dp2 = (grad * wl * slope(pre_second)).astype(BF)
    d_second = mm(h1, dp2, TN).astype(BF)
    for i in range(16):
        for h in range(2):
            d2[2 * i + h] = d_second[16 * i : 16 * i + 16, LANES * h : LANES * h + LANES]
    dp1 = (mm(dp2, w2_ref[...], NT) * slope(pre_hidden)).astype(BF)
    dpb[0] = dp1
    send(dpb.at[0], dpb.at[1], ps.at[1], pr.at[1], mate)
    send(d2.at[half], d2p, ps.at[2], pr.at[2], mate)

    dbil[...] = jnp.zeros_like(dbil)

    def fourth_pass(g, sums):
        u, sc = scaled_of(g)
        out = []
        for k, (v, vb, tot) in enumerate(((u, emb[rows256(g), :], total), (sc, flat(sc).astype(BF), total_s))):
            up = cube(mm(w1[rows256(k * groups + g), :], dp1, NT)) * FACTOR
            dq = up * cube(prod[k, rows256(g), :])
            dp = flat(up * (tot[None] - v)).astype(BF)
            du[k, rows256(g), :] = mm(kron, dp, NN) - flat(dq)
            dbil[...] += mm(vb, dp, NT)
            out.append(sums[k] + jnp.sum(dq, axis=0))
        return tuple(out)

    sum_q, sum_qs = lax.fori_loop(0, groups, fourth_pass, (zero, zero))

    got(jp, ps.at[0], pr.at[0], mate)
    got(dpb.at[1], ps.at[1], pr.at[1], mate)
    got(d2p, ps.at[2], pr.at[2], mate)
    both = dpb[...].reshape(2 * LANES, HID)

    def d_first_row(i):
        def one(k, _):
            q = i * SIDE + k
            left = jnp.concatenate([js[16 * c + q], jp[q]], axis=1)
            out = mm(left, both, NN).astype(BF)
            dfb[i, k, 0:LANES] = out[:, :LANES]
            dfb[i, k, LANES : 2 * LANES] = out[:, LANES:]
            dfb[i, k, 2 * LANES : BLOCK] = (d2[16 * c + q].astype(F32) + d2p[q].astype(F32)).astype(BF)
            return 0

        lax.fori_loop(0, SIDE, one, 0)

    for d in range(1, SIDE):
        i = lax.rem(a + d, SIDE)
        d_first_row(i)
        send(dfb.at[i], r1.at[a], s1.at[d], q1.at[a], {"tab": at(i, b)})
    d_first_row(a)

    def fifth_pass(g, _):
        u = cube(emb[rows256(g), :].astype(F32))
        w = wts[rows8(g), :]
        d_w = jnp.sum((cube(du[1, rows256(g), :]) + sum_qs[None]) * u, axis=1)
        dpw[rows8(g), :] = d_w * w * (1.0 - w)
        return 0

    lax.fori_loop(0, groups, fifth_pass, 0)
    d_pre_w = dpw[...]
    d_act = mm(sout_ref[...], d_pre_w, NN, HI) * slope(pre_one)
    dsq[...] = mm(sin_ref[...], d_act, NN, HI) * (1.0 / E)

    def sixth_pass(g, _):
        w = wts[rows8(g), :][:, None, :]
        out = cube(du[0, rows256(g), :]) + sum_q[None] + w * (cube(du[1, rows256(g), :]) + sum_qs[None])
        out = out + dsq[rows8(g), :][:, None, :]
        demb[rows8(g)] = out.astype(BF)
        return 0

    lax.fori_loop(0, groups, sixth_pass, 0)

    def by_slot(s, _):
        dslot[s] = demb[place_ref[s]]
        return 0

    lax.fori_loop(0, FIELDS, by_slot, 0)

    def d_send(i, _):
        p = lax.rem(t + i, TAB)
        send(dslot.at[pair(p)], rd_ref.at[pair(t)], ds.at[p], dr.at[t], {"tab": p})
        return 0

    lax.fori_loop(1, TAB, d_send, 0)
    rd_ref[pair(t)] = dslot[pair(t)]

    d_in = mm(squeeze, d_act, NT, HI)
    d_out = mm(act_one, d_pre_w, NT, HI)
    both_d = jnp.where(diag, dbil[...], 0.0)
    d_bil = mm(mm(small_cols.astype(F32), both_d, NN, HI), small_rows.astype(F32), NN, HI)
    sr[0, c] = jnp.zeros((SMALL, LANES), BF)
    sr[0, c, 0:FIELDS, 0:E] = d_in.astype(BF)
    sr[0, c, FIELDS : FIELDS + E, 0:FIELDS] = d_out.astype(BF)
    sr[0, c, FIELDS + E : FIELDS + 2 * E, 0:E] = d_bil.astype(BF)
    low = iota((16, LANES), 0)
    last = jnp.where(low == 0, d_last[:, :LANES], jnp.where(low == 1, d_last[:, LANES:], 0.0))
    sr[0, c, FIELDS + 2 * E : SMALL] = last.astype(BF)

    def peers(phase):
        if phase == 0:
            return c, [(1 - c, mate)]
        if phase == 1:
            return a, [(lax.rem(a + d, SIDE), {"tab": at(lax.rem(a + d, SIDE), b)}) for d in range(1, SIDE)]
        if phase == 2:
            return b, [(lax.rem(b + d, SIDE), {"tab": at(a, lax.rem(b + d, SIDE))}) for d in range(1, SIDE)]
        return r, [(lax.rem(r + d, REP), {"rep": lax.rem(r + d, REP)}) for d in range(1, REP)]

    def small_start(phase):
        me, others = peers(phase)
        for d, (_, dev) in enumerate(others):
            send(sr.at[phase, me], sr.at[phase, me], ss.at[phase, d], sq_r.at[phase, me], dev)

    def small_end(phase):
        me, others = peers(phase)
        for d, (who, dev) in enumerate(others):
            got(sr.at[phase, who], ss.at[phase, d], sq_r.at[phase, who], dev)
        size = 2 if phase == 0 else 4
        out = sr[phase, 0].astype(F32)
        for k in range(1, size):
            out = out + sr[phase, k].astype(F32)
        return out

    small_start(0)

    for d in range(1, SIDE):
        i = lax.rem(a + d, SIDE)
        got(r1.at[i], s1.at[d], q1.at[i], {"tab": at(i, b)})

    def first_sum(k, _):
        out = dfb[a, k].astype(F32)
        for d in range(1, SIDE):
            out = out + r1[lax.rem(a + d, SIDE), k].astype(F32)
        dfb[a, k] = out.astype(BF)
        return 0

    for d in range(1, SIDE):
        k = lax.rem(b + d, SIDE)
        first_sum(k, 0)
        send(dfb.at[a, k], r2.at[b], s2.at[d], q2.at[b], {"tab": at(a, k)})
    first_sum(b, 0)

    sr[1, a] = small_end(0).astype(BF)
    small_start(1)

    load_x.wait()

    def d_wait(i, _):
        p = lax.rem(t + i, TAB)
        got(rd_ref.at[pair(p)], ds.at[p], dr.at[p], {"tab": p})
        return 0

    lax.fori_loop(1, TAB, d_wait, 0)

    def proj_pass(j, acc):
        left = jnp.concatenate([rd_ref[pair(2 * j)].reshape(2 * E, LANES), rd_ref[pair(2 * j + 1)].reshape(2 * E, LANES)], axis=1)
        right = jnp.concatenate([xs[0, rows256(j), :], xs[1, rows256(j), :]], axis=1)
        return acc + mm(left, right, NN)

    acc = lax.fori_loop(0, TAB // 2, proj_pass, jnp.zeros((2 * E, 2 * LANES), F32))
    dz[r] = jnp.concatenate([acc[:E, :LANES], acc[E:, LANES:]], axis=0).astype(BF)
    for d in range(1, REP):
        o = lax.rem(r + d, REP)
        send(dz.at[r], dz.at[r], sd.at[d], qd.at[r], {"rep": o})

    sr[2, b] = small_end(1).astype(BF)
    small_start(2)

    for d in range(1, SIDE):
        k = lax.rem(b + d, SIDE)
        got(r2.at[k], s2.at[d], q2.at[k], {"tab": at(a, k)})
    out = dfb[a, b].astype(F32)
    for d in range(1, SIDE):
        out = out + r2[lax.rem(b + d, SIDE)].astype(F32)
    rz[r] = out.astype(BF)
    for d in range(1, REP):
        o = lax.rem(r + d, REP)
        send(rz.at[r], rz.at[r], sz.at[d], qz.at[r], {"rep": o})

    sr[3, r] = small_end(2).astype(BF)
    small_start(3)

    for d in range(1, REP):
        o = lax.rem(r + d, REP)
        got(rz.at[o], sz.at[d], qz.at[o], {"rep": o})
    out = rz[0].astype(F32)
    for k in range(1, REP):
        out = out + rz[k].astype(F32)
    df_ref[...] = out[: 2 * LANES]
    mine = block_of(t)
    ag_ref[mine] = out[2 * LANES :].astype(BF)

    def g_send(i, _):
        p = lax.rem(t + i, TAB)
        send(ag_ref.at[mine], ag_ref.at[mine], gs.at[p], gr.at[t], {"tab": p})
        return 0

    lax.fori_loop(1, TAB, g_send, 0)

    for d in range(1, REP):
        o = lax.rem(r + d, REP)
        got(dz.at[o], sd.at[d], qd.at[o], {"rep": o})
    out = dz[0].astype(F32)
    for k in range(1, REP):
        out = out + dz[k].astype(F32)
    dpt_ref[...] = out
    smf_ref[...] = small_end(3)

    def last_wait(i, _):
        p = lax.rem(t + i, TAB)
        dev = {"tab": p}
        got(lg_ref.at[p], ls.at[p], lr.at[p], dev)
        got(ag_ref.at[block_of(p)], gs.at[p], gr.at[p], dev)
        sent(e_ref.at[p], es.at[p], er.at[p], dev)
        sent(dslot.at[pair(p)], ds.at[p], dr.at[p], dev)
        sent(lg_ref.at[t], ls.at[p], lr.at[p], dev)
        sent(ag_ref.at[mine], gs.at[p], gr.at[p], dev)
        return 0

    lax.fori_loop(1, TAB, last_wait, 0)
    sent(js.at[half], ps.at[0], pr.at[0], mate)
    sent(dpb.at[0], ps.at[1], pr.at[1], mate)
    sent(d2.at[half], ps.at[2], pr.at[2], mate)
    for d in range(1, SIDE):
        i = lax.rem(a + d, SIDE)
        k = lax.rem(b + d, SIDE)
        o = lax.rem(r + d, REP)
        sent(dfb.at[i], s1.at[d], q1.at[i], {"tab": at(i, b)})
        sent(dfb.at[a, k], s2.at[d], q2.at[k], {"tab": at(a, k)})
        sent(rz.at[r], sz.at[d], qz.at[r], {"rep": o})
        sent(dz.at[r], sd.at[d], qd.at[r], {"rep": o})
    for phase in range(4):
        me, others = peers(phase)
        for d, (_, dev) in enumerate(others):
            sent(sr.at[phase, me], ss.at[phase, d], sq_r.at[phase, me], dev)


def exchange(inv, placement, e, labels, sin, sout, bil, w2, wl, w1, pooled):
    vmem = pl.BlockSpec(memory_space=pltpu.VMEM)
    smem = pl.BlockSpec(memory_space=pltpu.SMEM)
    hbm = pl.BlockSpec(memory_space=pl.ANY)
    rows = FIELDS * E
    dma = pltpu.SemaphoreType.DMA
    return pl.pallas_call(
        main_kernel,
        in_specs=[smem, smem] + [vmem] * 7 + [hbm, hbm],
        out_specs=[vmem] * 6,
        out_shape=[
            jax.ShapeDtypeStruct((FIELDS, E, LANES), BF),
            jax.ShapeDtypeStruct((TAB, 1, LANES), F32),
            jax.ShapeDtypeStruct((2 * LANES, LANES), F32),
            jax.ShapeDtypeStruct((TAB, 16, LANES), BF),
            jax.ShapeDtypeStruct((SMALL, LANES), F32),
            jax.ShapeDtypeStruct((2 * E, LANES), F32),
        ],
        scratch_shapes=[
            pltpu.VMEM(w1.shape, BF),
            pltpu.VMEM(pooled.shape, BF),
            pltpu.VMEM((FIELDS, E, LANES), BF),
            pltpu.VMEM((rows, LANES), BF),
            pltpu.VMEM((2, rows, LANES), F32),
            pltpu.VMEM((2, rows, LANES), F32),
            pltpu.VMEM((FIELDS, LANES), F32),
            pltpu.VMEM((FIELDS, LANES), F32),
            pltpu.VMEM((FIELDS, LANES), F32),
            pltpu.VMEM((FIELDS, LANES), F32),
            pltpu.VMEM((TAB, LANES, LANES), BF),
            pltpu.VMEM((16, LANES, LANES), BF),
            pltpu.VMEM((2, LANES, HID), BF),
            pltpu.VMEM((TAB, 16, LANES), BF),
            pltpu.VMEM((16, 16, LANES), BF),
            pltpu.VMEM((HID, HID), F32),
            pltpu.VMEM((FIELDS, E, LANES), BF),
            pltpu.VMEM((FIELDS, E, LANES), BF),
            pltpu.VMEM((SIDE, SIDE, BLOCK, LANES), BF),
            pltpu.VMEM((SIDE, SIDE, BLOCK, LANES), BF),
            pltpu.VMEM((SIDE, BLOCK, LANES), BF),
            pltpu.VMEM((REP, BLOCK, LANES), BF),
            pltpu.VMEM((4, 4, SMALL, LANES), BF),
            pltpu.VMEM((REP, 2 * E, LANES), BF),
            dma((2,)),
            dma((TAB,)), dma((TAB,)), dma((TAB,)), dma((TAB,)),
            dma((TAB,)), dma((TAB,)), dma((TAB,)), dma((TAB,)),
            dma((3,)), dma((3,)),
            dma((4,)), dma((4,)), dma((4,)), dma((4,)), dma((4,)), dma((4,)),
            dma((4, 4)), dma((4, 4)), dma((4,)), dma((4,)),
        ],
        compiler_params=pltpu.CompilerParams(
            collective_id=0, has_side_effects=True, vmem_limit_bytes=40 << 20
        ),
        name="exchange",
    )(inv, placement, e, labels, sin, sout, bil, w2, wl, w1, pooled)


def finish_kernel(
    tab_ref, rd_ref, pt_ref, mask_ref, lg_ref, df_ref, ag_ref, smf_ref, dpt_ref, route_ref,
    scores_ref, dx_ref, dproj_ref, din_ref, dout_ref, dbil_ref, dfirst_ref, dsecond_ref, dlast_ref,
):
    j = pl.program_id(0)
    pt = pt_ref[...]
    nil = jnp.zeros((E, LANES), BF)
    wide = jnp.concatenate(
        [jnp.concatenate([pt[:E], nil], axis=1), jnp.concatenate([nil, pt[E:]], axis=1)], axis=0
    )
    blocks = rd_ref.shape[0] // 2
    for k in range(blocks):
        out = mm(rd_ref[2 * k : 2 * k + 2].reshape(2 * E, LANES), wide, TN).astype(BF)
        dx_ref[0, k * LANES : (k + 1) * LANES] = out[:, :LANES]
        dx_ref[1, k * LANES : (k + 1) * LANES] = out[:, LANES:]

    @pl.when(j == 0)
    def _():
        idx = route_ref[:, pl.ds(pl.multiple_of(tab_ref[0] * LANES, LANES), LANES)]
        table = lg_ref[...].reshape(TAB, LANES)
        low = jnp.broadcast_to(lax.rem(idx, LANES), (TAB, LANES))
        found = jnp.take_along_axis(table, low, axis=1)
        scores_ref[...] = jnp.sum(
            jnp.where(idx // LANES == iota((TAB, LANES), 0), found, 0.0), axis=0, keepdims=True
        )
        eye = (iota((LANES, LANES), 0) == iota((LANES, LANES), 1)).astype(F32)
        kept = jnp.where(mask_ref[...] > 0, dpt_ref[...], 0.0)
        for s in range(2):
            dproj_ref[s] = mm(eye, kept[s * E : (s + 1) * E], NT, HI)
        din_ref[...] = smf_ref[0:FIELDS, 0:E]
        dout_ref[...] = smf_ref[FIELDS : FIELDS + E, 0:FIELDS]
        dbil_ref[...] = smf_ref[FIELDS + E : FIELDS + 2 * E, 0:E]
        dlast_ref[:, 0:LANES] = smf_ref[FIELDS + 2 * E : FIELDS + 2 * E + 1, :]
        dlast_ref[:, LANES:] = smf_ref[FIELDS + 2 * E + 1 : FIELDS + 2 * E + 2, :]
        dfirst_ref[:, 0:LANES] = df_ref[0:LANES, :]
        dfirst_ref[:, LANES:] = df_ref[LANES : 2 * LANES, :]
        for i in range(16):
            dsecond_ref[16 * i : 16 * i + 16, 0:LANES] = ag_ref[2 * i].astype(F32)
            dsecond_ref[16 * i : 16 * i + 16, LANES:] = ag_ref[2 * i + 1].astype(F32)


def finish(tab, rd, pt, mask, lg, df, ag, smf, dpt, route, pooled_shape):
    steps = 4
    rows = pooled_shape[1]
    chunk = rows // steps

    def whole(shape):
        return pl.BlockSpec(shape, lambda j, t: (0,) * len(shape))

    outs = [
        ((1, LANES), F32), (pooled_shape, BF), ((2, LANES, E), F32), ((FIELDS, E), F32), ((E, FIELDS), F32),
        ((E, E), F32), ((LANES, HID), F32), ((HID, HID), F32), ((1, HID), F32),
    ]
    out_specs = [whole(s) for s, _ in outs]
    out_specs[1] = pl.BlockSpec((2, chunk, LANES), lambda j, t: (0, j, 0))
    grid_spec = pltpu.PrefetchScalarGridSpec(
        num_scalar_prefetch=1,
        grid=(steps,),
        in_specs=[pl.BlockSpec((rd.shape[0] // steps, E, LANES), lambda j, t: (j, 0, 0))]
        + [whole(v.shape) for v in (pt, mask, lg, df, ag, smf, dpt, route)],
        out_specs=out_specs,
    )
    return pl.pallas_call(
        finish_kernel,
        grid_spec=grid_spec,
        out_shape=[jax.ShapeDtypeStruct(s, d) for s, d in outs],
        compiler_params=pltpu.CompilerParams(vmem_limit_bytes=16 << 20),
        name="finish",
    )(tab, rd, pt, mask, lg, df, ag, smf, dpt, route)


def shards(pooled, widths, placement, route, labels, proj, senet_in, senet_out, bilinear, w_first, w_second, w_last):
    tab = lax.axis_index("tab").astype(jnp.int32).reshape(1)
    e, pt, mask, inv = project(tab, placement, widths, pooled, proj)
    rd, lg, df, ag, smf, dpt = exchange(
        inv, placement, e, labels, senet_in, senet_out, bilinear, w_second, w_last[None, :], w_first, pooled
    )
    scores, dx, dproj, din, dout, dbil, dfirst, dsecond, dlast = finish(
        tab, rd, pt, mask, lg, df, ag, smf, dpt, route, pooled.shape
    )
    return scores, dx, dproj, din, dout, dbil, dfirst, dsecond, dlast[0]


def solution(mesh):
    whole = P()
    placed = (
        P("tab", "rep", None), whole, whole, P("rep", None), P("rep", None), whole, whole, whole, whole, whole,
        whole, whole,
    )
    return jax.shard_map(
        shards,
        mesh=mesh,
        in_specs=placed,
        out_specs=(
            P("rep", "tab"), P("tab", "rep", None), P("tab", None, None), whole, whole, whole, P("tab", None),
            whole, whole,
        ),
        check_vma=False,
    )
```

time: 226 us -> 79.6 us (0.35)
  Pallas kernels: 0 us -> 71.1 us
  blocking collectives: 69.8 us -> 0 us
  waiting for transfers between devices: 57.7 us -> 0 us
  starting transfers between devices: 25.7 us -> 0 us
  local copies, waits for them, and re-layouts: 29.1 us -> 6.47 us
  matrix products: 20.3 us -> 0 us
  between operations: 15.8 us -> 0.8 us
  other arithmetic: 6.22 us -> 0 us
    pallas_call x0 -> x3, Pallas kernels: none -> 71.1 us  [the longest x1 64.5 us: exchange(): pl.pallas_call(main_kernel, in_specs=[smem, smem] + [vmem] * 7 + [hbm, hb...]
    psum x1 -> x0, blocking collectives: 69.8 us -> none  [shards(): lax.psum((part_in, part_out, part_bil, part_second, part_last), ('tab', '...]
    psum x1 -> x0, waiting for transfers between devices: 39.3 us -> none  [shards(): lax.psum((part_in, part_out, part_bil, part_second, part_last), ('tab', '...]
    all_to_all x5 -> x0, starting transfers between devices: 25.6 us -> none  [the longest x3 10.8 us: sent_to_all(): lax.all_to_all(jnp.broadcast_to(value[None], (peers, *value.shape)), axis...]
    dot_general x23 -> x0, matrix products: 20.3 us -> none  [the longest x2 4.24 us: bilinear_backward(): d_fields = jnp.einsum('fnd,cd->fnc', d_product, bilinear)]
    all_to_all x5 -> x0, waiting for transfers between devices: 18.3 us -> none  [the longest x1 10.2 us: shards(): lax.all_to_all(embed_local, 'tab', split_axis=1, concat_axis=0, tiled=True)]
    unnamed x28 -> x24, local copies, waits for them, and re-layouts: 12.2 us -> 5.8 us
    gather x4 -> x0, local copies, waits for them, and re-layouts: 4.82 us -> none  [the longest x1 1.6 us: shards(): local_proj = jnp.take(proj, local_fields, axis=0)]
  transfers between devices with their start and end apart: 7 -> 0, of which waited for: 4 -> 0; matrix products, arithmetic and copies ran while one was open for 10% -> 0% of each run, Pallas kernels for 0% -> 0%
where the time goes in v1:
time: 79.6 us; the launch traced here: 78.4 us
  Pallas kernels  71.1 us (89%)
  local copies, waits for them, and re-layouts  6.47 us (8%)
  between operations  0.8 us (1%)
    pallas_call x1, Pallas kernels, exchange(): pl.pallas_call(main_kernel, in_specs=[smem, smem] + [vmem] * 7 + [hbm, hb...  64.5 us
    unnamed x24, local copies, waits for them, and re-layouts  5.8 us
    pallas_call x1, Pallas kernels, project(): pl.pallas_call(project_kernel, grid_spec=grid_spec, out_shape=[jax.ShapeD...  3.58 us
    pallas_call x1, Pallas kernels, finish(): pl.pallas_call(finish_kernel, grid_spec=grid_spec, out_shape=[jax.ShapeDt...  3.06 us

profile of v1, /device:TPU:0, one launch (start us, length us, event | category | flops | bytes accessed | tf_op | source)
XLA Modules:
  0.0 78.4 jit_solution(12179194381858529364)
XLA Ops:
  0.6 0.0 copy-start.8
  0.7 0.0 copy-start.9
  0.7 0.7 broadcast_in_dim.3.wl_ref
  1.3 0.8 %copy.22.sin_ref = f32[64,32]{1,0:T(8,128)S(1)} copy(f32[64,32]{0,1:T(8,128)} %param.18) | data formatting | bytes 16384 | tf_op args[6]
  2.1 0.0 copy-start.4
  2.1 0.0 copy-start.5
  2.2 0.0 copy-start.6
  2.2 2.0 %copy.21.proj_ref = bf16[64,128,32]{2,1,0:T(8,128)(2,1)S(1)} copy(bf16[64,128,32]{1,2,0:T(8,128)(2,1)} %param.17) | data formatting | bytes 1048576 | tf_op args[5]
  4.2 0.0 copy-done.8
  4.2 0.0 copy-done.9
  4.2 0.0 copy-start
  4.2 1.6 %copy-done = bf16[2,4096,128]{2,1,0:T(8,128)(2,1)S(1)} copy-done((bf16[2,4096,128]{2,1,0:T(8,128)(2,1)S(1)}, bf16[2,4096,128]{2,1,0:T(8,128)(2,1)}, u32[]{:S(2)}) %copy-start) | copy-done | bytes 2097176
  5.8 3.6 %project.1 = (bf16[32,2,32,128]{3,2,1,0:T(8,128)(2,1)S(1)}, bf16[64,128]{1,0:T(8,128)(2,1)S(1)}, f32[64,128]{1,0:T(8,128)S(1)}, s32[64]{0:T(128)S(1)}) custom-call(s32[1]{0:T(128)} %bitcast.tab_ref, s32[64]{0:T(128)S(1)} %copy-done.8, s32[64]{0:T(128)S(1)} %copy-done.9, bf16[2,4096,128]{2,1,0:T(8,128)(2,1)S(1)} %copy-done, ...), custom_call_target="tpu_custom_call" | custom-call | tf_op jit(solution)/shard_map/project/pallas_call | solution.py:84
  9.4 0.0 copy-done.3
  9.4 0.0 copy-done.4
  9.4 0.0 copy-done.5
  9.4 0.0 copy-done.6
  9.4 0.0 copy-done.1
  9.4 0.0 copy-done.2
  9.4 0.0 copy-start.7
  9.5 64.5 %exchange.1 = (bf16[64,32,128]{2,1,0:T(8,128)(2,1)S(1)}, f32[32,1,128]{2,1,0:T(1,128)S(1)}, f32[256,128]{1,0:T(8,128)S(1)}, bf16[32,16,128]{2,1,0:T(8,128)(2,1)S...) custom-call(s32[64]{0:T(128)S(1)} %get-tuple-element.28.inv_ref, s32[64]{0:T(128)S(1)} %copy-done.8, ...), custom_call_target="tpu_custom_call" | custom-call | tf_op jit(solution)/shard_map/exchange/pallas_call | solution.py:510
  74.0 3.1 %finish.1 = (f32[1,128]{1,0:T(1,128)}, bf16[2,4096,128]{2,1,0:T(8,128)(2,1)}, f32[2,128,32]{2,1,0:T(8,128)S(1)}, f32[64,32]{1,0:T(8,128)S(1)}, f32[32,64]{1,0:T(...) custom-call(s32[1]{0:T(128)} %bitcast.tab_ref, ...), custom_call_target="tpu_custom_call" | custom-call | tf_op jit(solution)/shard_map/finish/pallas_call | solution.py:623
  77.0 0.7 copy.24
  77.7 0.7 copy.23
  (4 shorter events, 0.0 us)
Async XLA Ops:
  0.6 3.5 %copy-start.8 = (s32[64]{0:T(128)S(1)}, s32[64]{0:T(128)}, u32[]{:S(2)}) copy-start(s32[64]{0:T(128)} %place_ref.3) | copy-start | bytes 772
  0.7 3.5 %copy-start.9 = (s32[64]{0:T(128)S(1)}, s32[64]{0:T(128)}, u32[]{:S(2)}) copy-start(s32[64]{0:T(128)} %width_ref.1) | copy-start | bytes 772
  2.1 7.3 %copy-start.3 = (bf16[256,256]{1,0:T(8,128)(2,1)S(1)}, bf16[256,256]{1,0:T(8,128)(2,1)}, u32[]{:S(2)}) copy-start(bf16[256,256]{1,0:T(8,128)(2,1)} %w2_ref.1) | copy-start | bytes 393220
  2.1 7.3 %copy-start.4 = (s32[1,4096]{1,0:T(1,128)S(1)}, s32[1,4096]{1,0:T(1,128)}, u32[]{:S(2)}) copy-start(s32[1,4096]{1,0:T(1,128)} %labels_ref.1) | copy-start | bytes 49156
  2.1 7.3 %copy-start.5 = (f32[32,64]{1,0:T(8,128)S(1)}, f32[32,64]{1,0:T(8,128)}, u32[]{:S(2)}) copy-start(f32[32,64]{1,0:T(8,128)} %sout_ref.1) | copy-start | bytes 24580
  2.2 7.3 %copy-start.6 = (f32[32,32]{1,0:T(8,128)S(1)}, f32[32,32]{1,0:T(8,128)}, u32[]{:S(2)}) copy-start(f32[32,32]{1,0:T(8,128)} %bil_ref.1) | copy-start | bytes 12292
  4.2 1.6 %copy-start = (bf16[2,4096,128]{2,1,0:T(8,128)(2,1)S(1)}, bf16[2,4096,128]{2,1,0:T(8,128)(2,1)}, u32[]{:S(2)}) copy-start(bf16[2,4096,128]{2,1,0:T(8,128)(2,1)} %pooled_hbm.1) | copy-start | bytes 6291460
  5.8 3.6 %copy-start.1 = (bf16[2,4096,128]{2,1,0:T(8,128)(2,1)S(1)}, bf16[2,4096,128]{2,1,0:T(8,128)(2,1)}, u32[]{:S(2)}) copy-start(bf16[2,4096,128]{2,1,0:T(8,128)(2,1)} %pooled_hbm.1) | copy-start | bytes 6291460
  5.8 3.6 %copy-start.2 = (bf16[4096,256]{1,0:T(8,128)(2,1)S(1)}, bf16[4096,256]{1,0:T(8,128)(2,1)}, u32[]{:S(2)}) copy-start(bf16[4096,256]{1,0:T(8,128)(2,1)} %w1_hbm.1) | copy-start | bytes 6291460
  9.4 64.5 %copy-start.7 = (s32[1,4096]{1,0:T(1,128)S(1)}, s32[1,4096]{1,0:T(1,128)}, u32[]{:S(2)}) copy-start(s32[1,4096]{1,0:T(1,128)} %route_ref.1) | copy-start | bytes 49156

commit v2 on v1

--- a/solution.py
+++ b/solution.py
@@ -18,11 +18,13 @@
 E = 32
 TAB = 32
 REP = 4
+EARLY = 4
 SIDE = 4
+PARTS = 4
 LANES = 128
 HID = 256
-BLOCK = 272
-SMALL = 144
+BLOCK = 256
+SMALL = 80
 FACTOR = 0.125
 
 
@@ -37,62 +39,6 @@
 
 def iota(shape, dim):
     return lax.broadcasted_iota(jnp.int32, shape, dim)
-
-
-def project_kernel(tab_ref, place_ref, width_ref, pooled_ref, proj_ref, e_ref, pt_ref, mask_ref, inv_ref):
-    i = pl.program_id(0)
-    j = pl.program_id(1)
-    field = place_ref[2 * tab_ref[0] + i]
-    width = width_ref[field]
-
-    @pl.when((i == 0) & (j == 0))
-    def _():
-        def put(s, _):
-            inv_ref[place_ref[s]] = s
-            return 0
-
-        lax.fori_loop(0, FIELDS, put, 0)
-
-    eye = (iota((E, E), 0) == iota((E, E), 1)).astype(BF)
-    keep = iota((E, LANES), 1) < width
-    turned = jnp.where(keep, mm(eye, proj_ref[0], NT), 0.0).astype(BF)
-    pt_ref[...] = turned
-    mask_ref[...] = keep.astype(F32)
-    out = mm(turned, pooled_ref[0], NT).astype(BF)
-    for d in range(out.shape[1] // LANES):
-        e_ref[d, 0] = out[:, d * LANES : (d + 1) * LANES]
-
-
-def project(tab, placement, widths, pooled, proj):
-    rows = pooled.shape[1]
-    steps = 2
-    chunk = rows // steps
-    grid_spec = pltpu.PrefetchScalarGridSpec(
-        num_scalar_prefetch=3,
-        grid=(2, steps),
-        in_specs=[
-            pl.BlockSpec((1, chunk, LANES), lambda i, j, t, p, w: (i, j, 0)),
-            pl.BlockSpec((1, LANES, E), lambda i, j, t, p, w: (p[2 * t[0] + i], 0, 0)),
-        ],
-        out_specs=[
-            pl.BlockSpec((chunk // LANES, 1, E, LANES), lambda i, j, t, p, w: (j, i, 0, 0)),
-            pl.BlockSpec((E, LANES), lambda i, j, t, p, w: (i, 0)),
-            pl.BlockSpec((E, LANES), lambda i, j, t, p, w: (i, 0)),
-            pl.BlockSpec(memory_space=pltpu.SMEM),
-        ],
-    )
-    return pl.pallas_call(
-        project_kernel,
-        grid_spec=grid_spec,
-        out_shape=[
-            jax.ShapeDtypeStruct((TAB, 2, E, LANES), BF),
-            jax.ShapeDtypeStruct((2 * E, LANES), BF),
-            jax.ShapeDtypeStruct((2 * E, LANES), F32),
-            jax.ShapeDtypeStruct((FIELDS,), jnp.int32),
-        ],
-        compiler_params=pltpu.CompilerParams(vmem_limit_bytes=16 << 20),
-        name="project",
-    )(tab, placement, widths, pooled, proj)
 
 
 def send(src, dst, ssem, rsem, dev):
@@ -117,10 +63,10 @@
 
 
 def main_kernel(
-    inv_ref, place_ref, e_ref, labels_ref, sin_ref, sout_ref, bil_ref, w2_ref, wl_ref, w1_hbm, pooled_hbm,
-    rd_ref, lg_ref, df_ref, ag_ref, smf_ref, dpt_ref,
-    w1, xs, recv, emb, prod, du, sq, wts, dpw, dsq, js, jp, dpb, d2, d2p, dbil, demb, dslot, dfb, r1, r2, rz, sr, dz,
-    load_sem, es, er, ds, dr, ls, lr, gs, gr, ps, pr, s1, q1, s2, q2, sz, qz, ss, sq_r, sd, qd,
+    inv_ref, place_ref, width_ref, labels_hbm, proj_hbm, sin_hbm, sout_hbm, bil_hbm, w1_hbm, w2_hbm, wl_hbm, pooled_hbm,
+    rd_ref, lg_ref, df_ref, ag_ref, smf_ref, dpt_ref, pt_ref,
+    labels_ref, projs, sin_ref, sout_ref, bil_ref, w1, w2_ref, wl_ref, xs, e_ref, recv, emb, prod, du, sq, wts, dpw, dsq, js, jp, dpb, d2, d2p, demb, dslot, dfb, r1, r2, rz, sr, dz, d2b, rd1, rd2, rdz,
+    load_sem, es, er, ds, dr, ls, lr, gs, gr, ps, pr, s1, q1, s2, q2, sz, qz, ss, sq_r, sd, qd, s1d, q1d, s2d, q2d, szd, qzd,
 ):
     t = lax.axis_index("tab")
     r = lax.axis_index("rep")
@@ -152,12 +98,34 @@
     for d in range(1, REP):
         pl.semaphore_signal(barrier, inc=1, device_id={"rep": lax.rem(r + d, REP)}, device_id_type=pl.DeviceIdType.MESH)
 
-    load_w1 = pltpu.make_async_copy(w1_hbm, w1, load_sem.at[0])
-    load_x = pltpu.make_async_copy(pooled_hbm, xs, load_sem.at[1])
-    load_w1.start()
-    load_x.start()
+    pairs = (
+        (proj_hbm, projs), (labels_hbm, labels_ref), (bil_hbm, bil_ref), (sin_hbm, sin_ref), (sout_hbm, sout_ref),
+        (w2_hbm, w2_ref), (wl_hbm, wl_ref), (w1_hbm, w1),
+    )
+    loads = [pltpu.make_async_copy(src, dst, load_sem.at[i]) for i, (src, dst) in enumerate(pairs)]
+    part = xs.shape[1] // PARTS
+    for k in range(PARTS):
+        piece = pl.ds(k * part, part)
+        loads.append(pltpu.make_async_copy(pooled_hbm.at[:, piece], xs.at[:, piece], load_sem.at[len(pairs) + k]))
+    for k in [0] + list(range(len(pairs), len(pairs) + PARTS)) + list(range(1, len(pairs))):
+        loads[k].start()
+
+    loads[0].wait()
+    keep = []
+    for i in range(2):
+        field = place_ref[2 * t + i]
+        keep.append(iota((E, LANES), 1) < width_ref[field])
+        pt_ref[i * E : (i + 1) * E, :] = jnp.where(keep[i], projs[field].astype(F32), 0.0).astype(BF)
+    for k in range(PARTS):
+        loads[len(pairs) + k].wait()
+        for i in range(2):
+            out = mm(pt_ref[i * E : (i + 1) * E, :], xs[i, k * part : (k + 1) * part, :], NT).astype(BF)
+            for d in range(part // LANES):
+                e_ref[k * (part // LANES) + d, i] = out[:, d * LANES : (d + 1) * LANES]
 
     small_rows = (lax.rem(iota((HID, E), 0), E) == iota((HID, E), 1)).astype(BF)
+    loads[1].wait()
+    loads[2].wait()
     small_cols = (lax.rem(iota((E, HID), 1), E) == iota((E, HID), 0)).astype(BF)
     diag = (iota((HID, HID), 0) // E) == (iota((HID, HID), 1) // E)
     bil = bil_ref[...].astype(BF)
@@ -220,7 +188,9 @@
     zero = jnp.zeros((E, LANES), F32)
     total = lax.fori_loop(0, groups, first_pass, zero)
     squeeze = sq[...]
-    pre_one = mm(sin_ref[...], squeeze, TN, HI)
+    loads[3].wait()
+    loads[4].wait()
+    pre_one = mm(sin_ref[...], squeeze, NN, HI)
     act_one = pre_one * jax.nn.sigmoid(pre_one)
     weights = jax.nn.sigmoid(mm(sout_ref[...], act_one, TN, HI))
     wts[...] = weights
@@ -234,7 +204,8 @@
 
     total_s = lax.fori_loop(0, groups, second_pass, zero)
 
-    load_w1.wait()
+    for k in range(5, len(pairs)):
+        loads[k].wait()
 
     def third_pass(g, acc):
         u, sc = scaled_of(g)
@@ -255,7 +226,7 @@
     h1 = (pre_hidden * jax.nn.sigmoid(pre_hidden)).astype(BF)
     pre_second = mm(h1, w2_ref[...], NN)
     h2 = (pre_second * jax.nn.sigmoid(pre_second)).astype(BF).astype(F32)
-    wl = wl_ref[...].astype(F32)
+    wl = wl_ref[...].reshape(1, HID).astype(F32)
     logit = jnp.sum(h2 * wl, axis=1, keepdims=True)
     lg_ref[t] = jnp.sum(jnp.where(square, logit, 0.0), axis=0, keepdims=True)
 
@@ -277,44 +248,75 @@
     send(dpb.at[0], dpb.at[1], ps.at[1], pr.at[1], mate)
     send(d2.at[half], d2p, ps.at[2], pr.at[2], mate)
 
-    dbil[...] = jnp.zeros_like(dbil)
+    def side(v):
+        return jnp.concatenate([v[i * E : (i + 1) * E] for i in range(8)], axis=1)
 
     def fourth_pass(g, sums):
         u, sc = scaled_of(g)
         out = []
+        bil_sum = sums[2]
         for k, (v, vb, tot) in enumerate(((u, emb[rows256(g), :], total), (sc, flat(sc).astype(BF), total_s))):
             up = cube(mm(w1[rows256(k * groups + g), :], dp1, NT)) * FACTOR
             dq = up * cube(prod[k, rows256(g), :])
             dp = flat(up * (tot[None] - v)).astype(BF)
             du[k, rows256(g), :] = mm(kron, dp, NN) - flat(dq)
-            dbil[...] += mm(vb, dp, NT)
+            bil_sum = bil_sum + mm(side(vb), side(dp), NT)
             out.append(sums[k] + jnp.sum(dq, axis=0))
-        return tuple(out)
-
-    sum_q, sum_qs = lax.fori_loop(0, groups, fourth_pass, (zero, zero))
+        return (*out, bil_sum)
+
+    sums = lax.fori_loop(0, EARLY, fourth_pass, (zero, zero, jnp.zeros((E, E), F32)))
+
+    def peer(me, d):
+        return lax.rem(me + d, SIDE)
 
     got(jp, ps.at[0], pr.at[0], mate)
     got(dpb.at[1], ps.at[1], pr.at[1], mate)
     got(d2p, ps.at[2], pr.at[2], mate)
+    d2b[...] = (d2[pl.ds(c * 16, 16)].astype(F32) + d2p[...].astype(F32)).astype(BF).reshape(d2b.shape)
+    for d in range(1, SIDE):
+        i = peer(a, d)
+        send(d2b.at[i], rd1.at[a], s1d.at[d], q1d.at[a], {"tab": at(i, b)})
+
     both = dpb[...].reshape(2 * LANES, HID)
 
     def d_first_row(i):
-        def one(k, _):
-            q = i * SIDE + k
-            left = jnp.concatenate([js[16 * c + q], jp[q]], axis=1)
-            out = mm(left, both, NN).astype(BF)
-            dfb[i, k, 0:LANES] = out[:, :LANES]
-            dfb[i, k, LANES : 2 * LANES] = out[:, LANES:]
-            dfb[i, k, 2 * LANES : BLOCK] = (d2[16 * c + q].astype(F32) + d2p[q].astype(F32)).astype(BF)
-            return 0
-
-        lax.fori_loop(0, SIDE, one, 0)
-
-    for d in range(1, SIDE):
-        i = lax.rem(a + d, SIDE)
+        left = jnp.concatenate(
+            [js[pl.ds(16 * c + i * SIDE, SIDE)].reshape(SIDE * LANES, LANES), jp[pl.ds(i * SIDE, SIDE)].reshape(SIDE * LANES, LANES)],
+            axis=1,
+        )
+        out = mm(left, both, NN).astype(BF)
+        for k in range(SIDE):
+            dfb[i, k, 0:LANES] = out[k * LANES : (k + 1) * LANES, :LANES]
+            dfb[i, k, LANES:] = out[k * LANES : (k + 1) * LANES, LANES:]
+
+    for d in range(1, SIDE):
+        i = peer(a, d)
         d_first_row(i)
         send(dfb.at[i], r1.at[a], s1.at[d], q1.at[a], {"tab": at(i, b)})
     d_first_row(a)
+
+    for d in range(1, SIDE):
+        i = peer(a, d)
+        got(rd1.at[i], s1d.at[d], q1d.at[i], {"tab": at(i, b)})
+    out = d2b[a].astype(F32)
+    for d in range(1, SIDE):
+        out = out + rd1[peer(a, d)].astype(F32)
+    d2b[a] = out.astype(BF)
+    for d in range(1, SIDE):
+        k = peer(b, d)
+        send(d2b.at[a, k], rd2.at[b], s2d.at[d], q2d.at[b], {"tab": at(a, k)})
+
+    sum_q, sum_qs, d_bil = lax.fori_loop(EARLY, groups, fourth_pass, sums)
+
+    for d in range(1, SIDE):
+        k = peer(b, d)
+        got(rd2.at[k], s2d.at[d], q2d.at[k], {"tab": at(a, k)})
+    out = d2b[a, b].astype(F32)
+    for d in range(1, SIDE):
+        out = out + rd2[peer(b, d)].astype(F32)
+    rdz[r] = out.astype(BF)
+    for d in range(1, REP):
+        send(rdz.at[r], rdz.at[r], szd.at[d], qzd.at[r], {"rep": peer(r, d)})
 
     def fifth_pass(g, _):
         u = cube(emb[rows256(g), :].astype(F32))
@@ -326,7 +328,7 @@
     lax.fori_loop(0, groups, fifth_pass, 0)
     d_pre_w = dpw[...]
     d_act = mm(sout_ref[...], d_pre_w, NN, HI) * slope(pre_one)
-    dsq[...] = mm(sin_ref[...], d_act, NN, HI) * (1.0 / E)
+    dsq[...] = mm(sin_ref[...], d_act, TN, HI) * (1.0 / E)
 
     def sixth_pass(g, _):
         w = wts[rows8(g), :][:, None, :]
@@ -351,17 +353,14 @@
     lax.fori_loop(1, TAB, d_send, 0)
     rd_ref[pair(t)] = dslot[pair(t)]
 
-    d_in = mm(squeeze, d_act, NT, HI)
+    d_in = mm(d_act, squeeze, NT, HI)
     d_out = mm(act_one, d_pre_w, NT, HI)
-    both_d = jnp.where(diag, dbil[...], 0.0)
-    d_bil = mm(mm(small_cols.astype(F32), both_d, NN, HI), small_rows.astype(F32), NN, HI)
-    sr[0, c] = jnp.zeros((SMALL, LANES), BF)
-    sr[0, c, 0:FIELDS, 0:E] = d_in.astype(BF)
-    sr[0, c, FIELDS : FIELDS + E, 0:FIELDS] = d_out.astype(BF)
-    sr[0, c, FIELDS + E : FIELDS + 2 * E, 0:E] = d_bil.astype(BF)
+    sr[0, c, 0:E] = jnp.concatenate([d_in, d_out], axis=1).astype(BF)
+    sr[0, c, E : 2 * E] = jnp.zeros((E, LANES), BF)
+    sr[0, c, E : 2 * E, 0:E] = d_bil.astype(BF)
     low = iota((16, LANES), 0)
     last = jnp.where(low == 0, d_last[:, :LANES], jnp.where(low == 1, d_last[:, LANES:], 0.0))
-    sr[0, c, FIELDS + 2 * E : SMALL] = last.astype(BF)
+    sr[0, c, 2 * E : SMALL] = last.astype(BF)
 
     def peers(phase):
         if phase == 0:
@@ -389,6 +388,21 @@
 
     small_start(0)
 
+    for d in range(1, REP):
+        got(rdz.at[peer(r, d)], szd.at[d], qzd.at[peer(r, d)], {"rep": peer(r, d)})
+    out = rdz[0].astype(F32)
+    for k in range(1, REP):
+        out = out + rdz[k].astype(F32)
+    mine = block_of(t)
+    ag_ref[mine] = out.astype(BF)
+
+    def g_send(i, _):
+        p = lax.rem(t + i, TAB)
+        send(ag_ref.at[mine], ag_ref.at[mine], gs.at[p], gr.at[t], {"tab": p})
+        return 0
+
+    lax.fori_loop(1, TAB, g_send, 0)
+
     for d in range(1, SIDE):
         i = lax.rem(a + d, SIDE)
         got(r1.at[i], s1.at[d], q1.at[i], {"tab": at(i, b)})
@@ -409,7 +423,6 @@
     sr[1, a] = small_end(0).astype(BF)
     small_start(1)
 
-    load_x.wait()
 
     def d_wait(i, _):
         p = lax.rem(t + i, TAB)
@@ -452,16 +465,7 @@
     out = rz[0].astype(F32)
     for k in range(1, REP):
         out = out + rz[k].astype(F32)
-    df_ref[...] = out[: 2 * LANES]
-    mine = block_of(t)
-    ag_ref[mine] = out[2 * LANES :].astype(BF)
-
-    def g_send(i, _):
-        p = lax.rem(t + i, TAB)
-        send(ag_ref.at[mine], ag_ref.at[mine], gs.at[p], gr.at[t], {"tab": p})
-        return 0
-
-    lax.fori_loop(1, TAB, g_send, 0)
+    df_ref[...] = out
 
     for d in range(1, REP):
         o = lax.rem(r + d, REP)
@@ -469,7 +473,8 @@
     out = dz[0].astype(F32)
     for k in range(1, REP):
         out = out + dz[k].astype(F32)
-    dpt_ref[...] = out
+    for i in range(2):
+        dpt_ref[i] = jnp.where(keep[i], out[i * E : (i + 1) * E], 0.0)
     smf_ref[...] = small_end(3)
 
     def last_wait(i, _):
@@ -494,6 +499,9 @@
         sent(dfb.at[i], s1.at[d], q1.at[i], {"tab": at(i, b)})
         sent(dfb.at[a, k], s2.at[d], q2.at[k], {"tab": at(a, k)})
         sent(rz.at[r], sz.at[d], qz.at[r], {"rep": o})
+        sent(d2b.at[i], s1d.at[d], q1d.at[i], {"tab": at(i, b)})
+        sent(d2b.at[a, k], s2d.at[d], q2d.at[k], {"tab": at(a, k)})
+        sent(rdz.at[r], szd.at[d], qzd.at[r], {"rep": o})
         sent(dz.at[r], sd.at[d], qd.at[r], {"rep": o})
     for phase in range(4):
         me, others = peers(phase)
@@ -501,27 +509,29 @@
             sent(sr.at[phase, me], ss.at[phase, d], sq_r.at[phase, me], dev)
 
 
-def exchange(inv, placement, e, labels, sin, sout, bil, w2, wl, w1, pooled):
+def exchange(inv, placement, widths, labels, proj, sin, sout, bil, w1, w2, wl, pooled):
     vmem = pl.BlockSpec(memory_space=pltpu.VMEM)
     smem = pl.BlockSpec(memory_space=pltpu.SMEM)
-    hbm = pl.BlockSpec(memory_space=pl.ANY)
+    hbm = pl.BlockSpec(memory_space=pltpu.HBM)
     rows = FIELDS * E
     dma = pltpu.SemaphoreType.DMA
+    arrays = (labels, proj, sin, sout, bil, w1, w2, wl, pooled)
     return pl.pallas_call(
         main_kernel,
-        in_specs=[smem, smem] + [vmem] * 7 + [hbm, hbm],
-        out_specs=[vmem] * 6,
+        in_specs=[smem] * 3 + [hbm] * len(arrays),
+        out_specs=[vmem] * 7,
         out_shape=[
             jax.ShapeDtypeStruct((FIELDS, E, LANES), BF),
             jax.ShapeDtypeStruct((TAB, 1, LANES), F32),
-            jax.ShapeDtypeStruct((2 * LANES, LANES), F32),
+            jax.ShapeDtypeStruct((BLOCK, LANES), F32),
             jax.ShapeDtypeStruct((TAB, 16, LANES), BF),
             jax.ShapeDtypeStruct((SMALL, LANES), F32),
-            jax.ShapeDtypeStruct((2 * E, LANES), F32),
+            jax.ShapeDtypeStruct((2, E, LANES), F32),
+            jax.ShapeDtypeStruct((2 * E, LANES), BF),
         ],
-        scratch_shapes=[
-            pltpu.VMEM(w1.shape, BF),
-            pltpu.VMEM(pooled.shape, BF),
+        scratch_shapes=[pltpu.VMEM(v.shape, v.dtype) for v in arrays]
+        + [
+            pltpu.VMEM((TAB, 2, E, LANES), BF),
             pltpu.VMEM((FIELDS, E, LANES), BF),
             pltpu.VMEM((rows, LANES), BF),
             pltpu.VMEM((2, rows, LANES), F32),
@@ -535,7 +545,6 @@
             pltpu.VMEM((2, LANES, HID), BF),
             pltpu.VMEM((TAB, 16, LANES), BF),
             pltpu.VMEM((16, 16, LANES), BF),
-            pltpu.VMEM((HID, HID), F32),
             pltpu.VMEM((FIELDS, E, LANES), BF),
             pltpu.VMEM((FIELDS, E, LANES), BF),
             pltpu.VMEM((SIDE, SIDE, BLOCK, LANES), BF),
@@ -544,22 +553,26 @@
             pltpu.VMEM((REP, BLOCK, LANES), BF),
             pltpu.VMEM((4, 4, SMALL, LANES), BF),
             pltpu.VMEM((REP, 2 * E, LANES), BF),
-            dma((2,)),
-            dma((TAB,)), dma((TAB,)), dma((TAB,)), dma((TAB,)),
-            dma((TAB,)), dma((TAB,)), dma((TAB,)), dma((TAB,)),
-            dma((3,)), dma((3,)),
-            dma((4,)), dma((4,)), dma((4,)), dma((4,)), dma((4,)), dma((4,)),
-            dma((4, 4)), dma((4, 4)), dma((4,)), dma((4,)),
-        ],
+            pltpu.VMEM((SIDE, SIDE, 16, LANES), BF),
+            pltpu.VMEM((SIDE, SIDE, 16, LANES), BF),
+            pltpu.VMEM((SIDE, 16, LANES), BF),
+            pltpu.VMEM((REP, 16, LANES), BF),
+            dma((8 + PARTS,)),
+        ]
+        + [dma((TAB,))] * 8
+        + [dma((3,))] * 2
+        + [dma((4,))] * 6
+        + [dma((4, 4))] * 2
+        + [dma((4,))] * 8,
         compiler_params=pltpu.CompilerParams(
-            collective_id=0, has_side_effects=True, vmem_limit_bytes=40 << 20
+            collective_id=0, has_side_effects=True, vmem_limit_bytes=60 * 1024 * 1024
         ),
         name="exchange",
-    )(inv, placement, e, labels, sin, sout, bil, w2, wl, w1, pooled)
+    )(inv, placement, widths, *arrays)
 
 
 def finish_kernel(
-    tab_ref, rd_ref, pt_ref, mask_ref, lg_ref, df_ref, ag_ref, smf_ref, dpt_ref, route_ref,
+    tab_ref, rd_ref, pt_ref, lg_ref, df_ref, ag_ref, smf_ref, dpt_ref, route_ref,
     scores_ref, dx_ref, dproj_ref, din_ref, dout_ref, dbil_ref, dfirst_ref, dsecond_ref, dlast_ref,
 ):
     j = pl.program_id(0)
@@ -583,15 +596,12 @@
         scores_ref[...] = jnp.sum(
             jnp.where(idx // LANES == iota((TAB, LANES), 0), found, 0.0), axis=0, keepdims=True
         )
-        eye = (iota((LANES, LANES), 0) == iota((LANES, LANES), 1)).astype(F32)
-        kept = jnp.where(mask_ref[...] > 0, dpt_ref[...], 0.0)
-        for s in range(2):
-            dproj_ref[s] = mm(eye, kept[s * E : (s + 1) * E], NT, HI)
-        din_ref[...] = smf_ref[0:FIELDS, 0:E]
-        dout_ref[...] = smf_ref[FIELDS : FIELDS + E, 0:FIELDS]
-        dbil_ref[...] = smf_ref[FIELDS + E : FIELDS + 2 * E, 0:E]
-        dlast_ref[:, 0:LANES] = smf_ref[FIELDS + 2 * E : FIELDS + 2 * E + 1, :]
-        dlast_ref[:, LANES:] = smf_ref[FIELDS + 2 * E + 1 : FIELDS + 2 * E + 2, :]
+        dproj_ref[...] = dpt_ref[...]
+        din_ref[...] = smf_ref[0:E, 0:FIELDS]
+        dout_ref[...] = smf_ref[0:E, FIELDS:]
+        dbil_ref[...] = smf_ref[E : 2 * E, 0:E]
+        dlast_ref[:, 0:LANES] = smf_ref[2 * E : 2 * E + 1, :]
+        dlast_ref[:, LANES:] = smf_ref[2 * E + 1 : 2 * E + 2, :]
         dfirst_ref[:, 0:LANES] = df_ref[0:LANES, :]
         dfirst_ref[:, LANES:] = df_ref[LANES : 2 * LANES, :]
         for i in range(16):
@@ -599,7 +609,7 @@
             dsecond_ref[16 * i : 16 * i + 16, LANES:] = ag_ref[2 * i + 1].astype(F32)
 
 
-def finish(tab, rd, pt, mask, lg, df, ag, smf, dpt, route, pooled_shape):
+def finish(tab, rd, pt, lg, df, ag, smf, dpt, route, pooled_shape):
     steps = 4
     rows = pooled_shape[1]
     chunk = rows // steps
@@ -608,7 +618,7 @@
         return pl.BlockSpec(shape, lambda j, t: (0,) * len(shape))
 
     outs = [
-        ((1, LANES), F32), (pooled_shape, BF), ((2, LANES, E), F32), ((FIELDS, E), F32), ((E, FIELDS), F32),
+        ((1, LANES), F32), (pooled_shape, BF), ((2, E, LANES), F32), ((E, FIELDS), F32), ((E, FIELDS), F32),
         ((E, E), F32), ((LANES, HID), F32), ((HID, HID), F32), ((1, HID), F32),
     ]
     out_specs = [whole(s) for s, _ in outs]
@@ -617,28 +627,30 @@
         num_scalar_prefetch=1,
         grid=(steps,),
         in_specs=[pl.BlockSpec((rd.shape[0] // steps, E, LANES), lambda j, t: (j, 0, 0))]
-        + [whole(v.shape) for v in (pt, mask, lg, df, ag, smf, dpt, route)],
+        + [whole(v.shape) for v in (pt, lg, df, ag, smf, dpt, route)],
         out_specs=out_specs,
     )
     return pl.pallas_call(
         finish_kernel,
         grid_spec=grid_spec,
         out_shape=[jax.ShapeDtypeStruct(s, d) for s, d in outs],
-        compiler_params=pltpu.CompilerParams(vmem_limit_bytes=16 << 20),
+        compiler_params=pltpu.CompilerParams(vmem_limit_bytes=60 * 1024 * 1024),
         name="finish",
-    )(tab, rd, pt, mask, lg, df, ag, smf, dpt, route)
+    )(tab, rd, pt, lg, df, ag, smf, dpt, route)
 
 
 def shards(pooled, widths, placement, route, labels, proj, senet_in, senet_out, bilinear, w_first, w_second, w_last):
     tab = lax.axis_index("tab").astype(jnp.int32).reshape(1)
-    e, pt, mask, inv = project(tab, placement, widths, pooled, proj)
-    rd, lg, df, ag, smf, dpt = exchange(
-        inv, placement, e, labels, senet_in, senet_out, bilinear, w_second, w_last[None, :], w_first, pooled
+    fields = jnp.arange(FIELDS, dtype=jnp.int32)
+    inv = jnp.sum(jnp.where(placement[:, None] == fields[None, :], fields[:, None], 0), axis=0)
+    rd, lg, df, ag, smf, dpt, pt = exchange(
+        inv, placement, widths, labels, jnp.swapaxes(proj, 1, 2), senet_in.T, senet_out, bilinear, w_first, w_second,
+        w_last, pooled,
     )
     scores, dx, dproj, din, dout, dbil, dfirst, dsecond, dlast = finish(
-        tab, rd, pt, mask, lg, df, ag, smf, dpt, route, pooled.shape
+        tab, rd, pt, lg, df, ag, smf, dpt, route, pooled.shape
     )
-    return scores, dx, dproj, din, dout, dbil, dfirst, dsecond, dlast[0]
+    return scores, dx, jnp.swapaxes(dproj, 1, 2), din.T, dout, dbil, dfirst, dsecond, dlast[0]
 
 
 def solution(mesh):

time: 79.6 us -> 66.5 us (0.84); the launches traced: 78.4 us -> 66.3 us
  Pallas kernels: 71.1 us -> 64.4 us
  local copies, waits for them, and re-layouts: 6.47 us -> 0 us
  other arithmetic: 0 us -> 1.26 us
    pallas_call x2 -> x1, Pallas kernels: 68.1 us -> 59.9 us  [exchange(): pl.pallas_call(main_kernel, in_specs=[smem] * 3 + [hbm] * len(arrays), ou...]
    unnamed x24 -> x0, local copies, waits for them, and re-layouts: 5.8 us -> none
    pallas_call x1, Pallas kernels: 3.06 us -> 4.55 us  [finish(): pl.pallas_call(finish_kernel, grid_spec=grid_spec, out_shape=[jax.ShapeDt...]
    reduce_sum x0 -> x1, other arithmetic: none -> 1.26 us  [shards(): jnp.sum(jnp.where(placement[:, None] == fields[None, :], fields[:, None],...]
where the time goes in v2:
time: 66.5 us; the launch traced here: 66.3 us
  Pallas kernels  64.4 us (97%)
  other arithmetic  1.26 us (2%)
    pallas_call x1, Pallas kernels, exchange(): pl.pallas_call(main_kernel, in_specs=[smem] * 3 + [hbm] * len(arrays), ou...  59.9 us
    pallas_call x1, Pallas kernels, finish(): pl.pallas_call(finish_kernel, grid_spec=grid_spec, out_shape=[jax.ShapeDt...  4.55 us

profile of v2, /device:TPU:0, one launch (start us, length us, event | category | flops | bytes accessed | tf_op | source)
XLA Modules:
  0.0 66.3 jit_solution(5513640216115392960)
XLA Ops:
  0.6 1.3 %select_reduce_fusion.inv_ref = s32[64]{0:T(128)} fusion(s32[64]{0:T(128)} %place_ref.1), kind=kLoop, calls=%fused_computation | loop fusion | flops 12224 | bytes 512 | tf_op jit(solution)/shard_map/reduce_sum | solution.py:645
  1.9 59.9 %exchange.1 = (bf16[64,32,128]{2,1,0:T(8,128)(2,1)}, f32[32,1,128]{2,1,0:T(1,128)}, f32[256,128]{1,0:T(8,128)}, bf16[32,16,128]{2,1,0:T(8,128)(2,1)}, f32[80,128...) custom-call(s32[64]{0:T(128)} %select_reduce_fusion.inv_ref, s32[64]{0:T(128)} %place_ref.1, s32[64]{0:T(128)} %width_ref.1, ...), custom_call_target="tpu_custom_call" | custom-call | tf_op jit(solution)/shard_map/exchange/pallas_call | solution.py:519
  61.8 4.5 %finish.1 = (f32[1,128]{1,0:T(1,128)}, bf16[2,4096,128]{2,1,0:T(8,128)(2,1)}, f32[2,32,128]{2,1,0:T(8,128)}, f32[32,64]{1,0:T(8,128)}, f32[32,64]{1,0:T(8,128)},...) custom-call(s32[1]{0:T(128)} %bitcast.tab_ref, ...), custom_call_target="tpu_custom_call" | custom-call | tf_op jit(solution)/shard_map/finish/pallas_call | solution.py:633

commit v3 on v2

--- a/solution.py
+++ b/solution.py
@@ -63,9 +63,9 @@
 
 
 def main_kernel(
-    inv_ref, place_ref, width_ref, labels_hbm, proj_hbm, sin_hbm, sout_hbm, bil_hbm, w1_hbm, w2_hbm, wl_hbm, pooled_hbm,
+    place_ref, width_ref, place_hbm, labels_hbm, proj_hbm, sin_hbm, sout_hbm, bil_hbm, w1_hbm, w2_hbm, wl_hbm, pooled_hbm,
     rd_ref, lg_ref, df_ref, ag_ref, smf_ref, dpt_ref, pt_ref,
-    labels_ref, projs, sin_ref, sout_ref, bil_ref, w1, w2_ref, wl_ref, xs, e_ref, recv, emb, prod, du, sq, wts, dpw, dsq, js, jp, dpb, d2, d2p, demb, dslot, dfb, r1, r2, rz, sr, dz, d2b, rd1, rd2, rdz,
+    place_vec, labels_ref, projs, sin_ref, sout_ref, bil_ref, w1, w2_ref, wl_ref, xs, e_ref, recv, emb, prod, du, sq, wts, dpw, dsq, js, jp, dpb, d2, d2p, demb, dslot, dfb, r1, r2, rz, sr, dz, d2b, rd1, rd2, rdz, inv_vec, inv_ref,
     load_sem, es, er, ds, dr, ls, lr, gs, gr, ps, pr, s1, q1, s2, q2, sz, qz, ss, sq_r, sd, qd, s1d, q1d, s2d, q2d, szd, qzd,
 ):
     t = lax.axis_index("tab")
@@ -100,15 +100,25 @@
 
     pairs = (
         (proj_hbm, projs), (labels_hbm, labels_ref), (bil_hbm, bil_ref), (sin_hbm, sin_ref), (sout_hbm, sout_ref),
-        (w2_hbm, w2_ref), (wl_hbm, wl_ref), (w1_hbm, w1),
+        (w2_hbm, w2_ref), (wl_hbm, wl_ref), (w1_hbm, w1), (place_hbm, place_vec),
     )
     loads = [pltpu.make_async_copy(src, dst, load_sem.at[i]) for i, (src, dst) in enumerate(pairs)]
     part = xs.shape[1] // PARTS
     for k in range(PARTS):
         piece = pl.ds(k * part, part)
         loads.append(pltpu.make_async_copy(pooled_hbm.at[:, piece], xs.at[:, piece], load_sem.at[len(pairs) + k]))
-    for k in [0] + list(range(len(pairs), len(pairs) + PARTS)) + list(range(1, len(pairs))):
+    for k in [8, 0] + list(range(len(pairs), len(pairs) + PARTS)) + list(range(1, 8)):
         loads[k].start()
+
+    loads[8].wait()
+    line = place_vec[...].reshape(1, FIELDS)
+    eye = iota((FIELDS, FIELDS), 0) == iota((FIELDS, FIELDS), 1)
+    column = jnp.sum(jnp.where(eye, line, 0), axis=1, keepdims=True)
+    spots = iota((FIELDS, FIELDS), 0)
+    slot_of = jnp.sum(jnp.where(column == iota((FIELDS, FIELDS), 1), spots, 0), axis=0, keepdims=True)
+    inv_vec[...] = jnp.minimum(slot_of, FIELDS - 1)
+    invert = pltpu.make_async_copy(inv_vec, inv_ref, load_sem.at[9 + PARTS])
+    invert.start()
 
     loads[0].wait()
     keep = []
@@ -160,11 +170,13 @@
     def rows32(f):
         return pl.ds(pl.multiple_of(f * E, E), E)
 
+    invert.wait()
+
     def by_field(f, _):
-        emb[rows32(f), :] = recv[inv_ref[f]]
-        return 0
-
-    lax.fori_loop(0, FIELDS, by_field, 0)
+        emb[rows32(f), :] = recv[inv_ref[0, f]]
+        return 0
+
+    lax.fori_loop(0, FIELDS, by_field, 0, unroll=16)
 
     groups = FIELDS // 8
 
@@ -186,7 +198,7 @@
         return total + jnp.sum(u, axis=0)
 
     zero = jnp.zeros((E, LANES), F32)
-    total = lax.fori_loop(0, groups, first_pass, zero)
+    total = lax.fori_loop(0, groups, first_pass, zero, unroll=8)
     squeeze = sq[...]
     loads[3].wait()
     loads[4].wait()
@@ -202,9 +214,9 @@
     def second_pass(g, tot):
         return tot + jnp.sum(scaled_of(g)[1], axis=0)
 
-    total_s = lax.fori_loop(0, groups, second_pass, zero)
-
-    for k in range(5, len(pairs)):
+    total_s = lax.fori_loop(0, groups, second_pass, zero, unroll=8)
+
+    for k in range(5, 8):
         loads[k].wait()
 
     def third_pass(g, acc):
@@ -219,7 +231,7 @@
             acc = acc + mm(j, w1[rows256(k * groups + g), :], TN)
         return acc
 
-    pre_hidden = lax.fori_loop(0, groups, third_pass, jnp.zeros((LANES, HID), F32))
+    pre_hidden = lax.fori_loop(0, groups, third_pass, jnp.zeros((LANES, HID), F32), unroll=8)
     half = pl.ds((1 - c) * 16, 16)
     send(js.at[half], jp, ps.at[0], pr.at[0], mate)
 
@@ -264,7 +276,7 @@
             out.append(sums[k] + jnp.sum(dq, axis=0))
         return (*out, bil_sum)
 
-    sums = lax.fori_loop(0, EARLY, fourth_pass, (zero, zero, jnp.zeros((E, E), F32)))
+    sums = lax.fori_loop(0, EARLY, fourth_pass, (zero, zero, jnp.zeros((E, E), F32)), unroll=4)
 
     def peer(me, d):
         return lax.rem(me + d, SIDE)
@@ -306,7 +318,7 @@
         k = peer(b, d)
         send(d2b.at[a, k], rd2.at[b], s2d.at[d], q2d.at[b], {"tab": at(a, k)})
 
-    sum_q, sum_qs, d_bil = lax.fori_loop(EARLY, groups, fourth_pass, sums)
+    sum_q, sum_qs, d_bil = lax.fori_loop(EARLY, groups, fourth_pass, sums, unroll=4)
 
     for d in range(1, SIDE):
         k = peer(b, d)
@@ -325,7 +337,7 @@
         dpw[rows8(g), :] = d_w * w * (1.0 - w)
         return 0
 
-    lax.fori_loop(0, groups, fifth_pass, 0)
+    lax.fori_loop(0, groups, fifth_pass, 0, unroll=8)
     d_pre_w = dpw[...]
     d_act = mm(sout_ref[...], d_pre_w, NN, HI) * slope(pre_one)
     dsq[...] = mm(sin_ref[...], d_act, TN, HI) * (1.0 / E)
@@ -337,13 +349,13 @@
         demb[rows8(g)] = out.astype(BF)
         return 0
 
-    lax.fori_loop(0, groups, sixth_pass, 0)
+    lax.fori_loop(0, groups, sixth_pass, 0, unroll=8)
 
     def by_slot(s, _):
         dslot[s] = demb[place_ref[s]]
         return 0
 
-    lax.fori_loop(0, FIELDS, by_slot, 0)
+    lax.fori_loop(0, FIELDS, by_slot, 0, unroll=16)
 
     def d_send(i, _):
         p = lax.rem(t + i, TAB)
@@ -436,7 +448,7 @@
         right = jnp.concatenate([xs[0, rows256(j), :], xs[1, rows256(j), :]], axis=1)
         return acc + mm(left, right, NN)
 
-    acc = lax.fori_loop(0, TAB // 2, proj_pass, jnp.zeros((2 * E, 2 * LANES), F32))
+    acc = lax.fori_loop(0, TAB // 2, proj_pass, jnp.zeros((2 * E, 2 * LANES), F32), unroll=8)
     dz[r] = jnp.concatenate([acc[:E, :LANES], acc[E:, LANES:]], axis=0).astype(BF)
     for d in range(1, REP):
         o = lax.rem(r + d, REP)
@@ -509,16 +521,16 @@
             sent(sr.at[phase, me], ss.at[phase, d], sq_r.at[phase, me], dev)
 
 
-def exchange(inv, placement, widths, labels, proj, sin, sout, bil, w1, w2, wl, pooled):
+def exchange(placement, widths, labels, proj, sin, sout, bil, w1, w2, wl, pooled):
     vmem = pl.BlockSpec(memory_space=pltpu.VMEM)
     smem = pl.BlockSpec(memory_space=pltpu.SMEM)
     hbm = pl.BlockSpec(memory_space=pltpu.HBM)
     rows = FIELDS * E
     dma = pltpu.SemaphoreType.DMA
-    arrays = (labels, proj, sin, sout, bil, w1, w2, wl, pooled)
+    arrays = (placement, labels, proj, sin, sout, bil, w1, w2, wl, pooled)
     return pl.pallas_call(
         main_kernel,
-        in_specs=[smem] * 3 + [hbm] * len(arrays),
+        in_specs=[smem] * 2 + [hbm] * len(arrays),
         out_specs=[vmem] * 7,
         out_shape=[
             jax.ShapeDtypeStruct((FIELDS, E, LANES), BF),
@@ -557,7 +569,9 @@
             pltpu.VMEM((SIDE, SIDE, 16, LANES), BF),
             pltpu.VMEM((SIDE, 16, LANES), BF),
             pltpu.VMEM((REP, 16, LANES), BF),
-            dma((8 + PARTS,)),
+            pltpu.VMEM((1, FIELDS), jnp.int32),
+            pltpu.SMEM((1, FIELDS), jnp.int32),
+            dma((10 + PARTS,)),
         ]
         + [dma((TAB,))] * 8
         + [dma((3,))] * 2
@@ -568,83 +582,91 @@
             collective_id=0, has_side_effects=True, vmem_limit_bytes=60 * 1024 * 1024
         ),
         name="exchange",
-    )(inv, placement, widths, *arrays)
+    )(placement, widths, *arrays)
 
 
 def finish_kernel(
-    tab_ref, rd_ref, pt_ref, lg_ref, df_ref, ag_ref, smf_ref, dpt_ref, route_ref,
-    scores_ref, dx_ref, dproj_ref, din_ref, dout_ref, dbil_ref, dfirst_ref, dsecond_ref, dlast_ref,
+    tab_ref, rd_hbm, pt_hbm, lg_hbm, df_hbm, ag_hbm, smf_hbm, dpt_hbm, route_hbm,
+    scores_ref, dx_hbm, dproj_ref, din_ref, dout_ref, dbil_ref, dfirst_ref, dsecond_ref, dlast_ref,
+    rd_ref, pt_ref, lg_ref, df_ref, ag_ref, smf_ref, route_ref, dx, load_sem, out_sem,
 ):
-    j = pl.program_id(0)
+    pairs = (
+        (rd_hbm, rd_ref), (pt_hbm, pt_ref), (lg_hbm, lg_ref), (route_hbm, route_ref), (smf_hbm, smf_ref),
+        (df_hbm, df_ref), (ag_hbm, ag_ref), (dpt_hbm, dproj_ref),
+    )
+    loads = [pltpu.make_async_copy(src, dst, load_sem.at[i]) for i, (src, dst) in enumerate(pairs)]
+    for k in (1, 0, 2, 3, 4, 5, 6, 7):
+        loads[k].start()
+    loads[1].wait()
     pt = pt_ref[...]
     nil = jnp.zeros((E, LANES), BF)
     wide = jnp.concatenate(
         [jnp.concatenate([pt[:E], nil], axis=1), jnp.concatenate([nil, pt[E:]], axis=1)], axis=0
     )
-    blocks = rd_ref.shape[0] // 2
-    for k in range(blocks):
-        out = mm(rd_ref[2 * k : 2 * k + 2].reshape(2 * E, LANES), wide, TN).astype(BF)
-        dx_ref[0, k * LANES : (k + 1) * LANES] = out[:, :LANES]
-        dx_ref[1, k * LANES : (k + 1) * LANES] = out[:, LANES:]
-
-    @pl.when(j == 0)
-    def _():
-        idx = route_ref[:, pl.ds(pl.multiple_of(tab_ref[0] * LANES, LANES), LANES)]
-        table = lg_ref[...].reshape(TAB, LANES)
-        low = jnp.broadcast_to(lax.rem(idx, LANES), (TAB, LANES))
-        found = jnp.take_along_axis(table, low, axis=1)
-        scores_ref[...] = jnp.sum(
-            jnp.where(idx // LANES == iota((TAB, LANES), 0), found, 0.0), axis=0, keepdims=True
-        )
-        dproj_ref[...] = dpt_ref[...]
-        din_ref[...] = smf_ref[0:E, 0:FIELDS]
-        dout_ref[...] = smf_ref[0:E, FIELDS:]
-        dbil_ref[...] = smf_ref[E : 2 * E, 0:E]
-        dlast_ref[:, 0:LANES] = smf_ref[2 * E : 2 * E + 1, :]
-        dlast_ref[:, LANES:] = smf_ref[2 * E + 1 : 2 * E + 2, :]
-        dfirst_ref[:, 0:LANES] = df_ref[0:LANES, :]
-        dfirst_ref[:, LANES:] = df_ref[LANES : 2 * LANES, :]
-        for i in range(16):
-            dsecond_ref[16 * i : 16 * i + 16, 0:LANES] = ag_ref[2 * i].astype(F32)
-            dsecond_ref[16 * i : 16 * i + 16, LANES:] = ag_ref[2 * i + 1].astype(F32)
+    loads[0].wait()
+    part = dx.shape[1] // PARTS
+    writes = []
+    for p in range(PARTS):
+        for k in range(p * (TAB // PARTS), (p + 1) * (TAB // PARTS)):
+            out = mm(rd_ref[2 * k : 2 * k + 2].reshape(2 * E, LANES), wide, TN).astype(BF)
+            dx[0, k * LANES : (k + 1) * LANES] = out[:, :LANES]
+            dx[1, k * LANES : (k + 1) * LANES] = out[:, LANES:]
+        piece = pl.ds(p * part, part)
+        writes.append(pltpu.make_async_copy(dx.at[:, piece], dx_hbm.at[:, piece], out_sem.at[p]))
+        writes[p].start()
+
+    for k in range(2, len(pairs)):
+        loads[k].wait()
+    idx = route_ref[:, pl.ds(pl.multiple_of(tab_ref[0] * LANES, LANES), LANES)]
+    table = lg_ref[...].reshape(TAB, LANES)
+    low = jnp.broadcast_to(lax.rem(idx, LANES), (TAB, LANES))
+    found = jnp.take_along_axis(table, low, axis=1)
+    scores_ref[...] = jnp.sum(
+        jnp.where(idx // LANES == iota((TAB, LANES), 0), found, 0.0), axis=0, keepdims=True
+    )
+    din_ref[...] = smf_ref[0:E, 0:FIELDS]
+    dout_ref[...] = smf_ref[0:E, FIELDS:]
+    dbil_ref[...] = smf_ref[E : 2 * E, 0:E]
+    dlast_ref[:, 0:LANES] = smf_ref[2 * E : 2 * E + 1, :]
+    dlast_ref[:, LANES:] = smf_ref[2 * E + 1 : 2 * E + 2, :]
+    dfirst_ref[:, 0:LANES] = df_ref[0:LANES, :]
+    dfirst_ref[:, LANES:] = df_ref[LANES : 2 * LANES, :]
+    for i in range(16):
+        dsecond_ref[16 * i : 16 * i + 16, 0:LANES] = ag_ref[2 * i].astype(F32)
+        dsecond_ref[16 * i : 16 * i + 16, LANES:] = ag_ref[2 * i + 1].astype(F32)
+    for w in writes:
+        w.wait()
 
 
 def finish(tab, rd, pt, lg, df, ag, smf, dpt, route, pooled_shape):
-    steps = 4
-    rows = pooled_shape[1]
-    chunk = rows // steps
-
-    def whole(shape):
-        return pl.BlockSpec(shape, lambda j, t: (0,) * len(shape))
-
+    vmem = pl.BlockSpec(memory_space=pltpu.VMEM)
+    smem = pl.BlockSpec(memory_space=pltpu.SMEM)
+    hbm = pl.BlockSpec(memory_space=pltpu.HBM)
+    arrays = (rd, pt, lg, df, ag, smf, dpt, route)
     outs = [
         ((1, LANES), F32), (pooled_shape, BF), ((2, E, LANES), F32), ((E, FIELDS), F32), ((E, FIELDS), F32),
         ((E, E), F32), ((LANES, HID), F32), ((HID, HID), F32), ((1, HID), F32),
     ]
-    out_specs = [whole(s) for s, _ in outs]
-    out_specs[1] = pl.BlockSpec((2, chunk, LANES), lambda j, t: (0, j, 0))
-    grid_spec = pltpu.PrefetchScalarGridSpec(
-        num_scalar_prefetch=1,
-        grid=(steps,),
-        in_specs=[pl.BlockSpec((rd.shape[0] // steps, E, LANES), lambda j, t: (j, 0, 0))]
-        + [whole(v.shape) for v in (pt, lg, df, ag, smf, dpt, route)],
-        out_specs=out_specs,
-    )
     return pl.pallas_call(
         finish_kernel,
-        grid_spec=grid_spec,
+        in_specs=[smem] + [hbm] * len(arrays),
+        out_specs=[vmem, hbm] + [vmem] * 7,
         out_shape=[jax.ShapeDtypeStruct(s, d) for s, d in outs],
+        scratch_shapes=[pltpu.VMEM(v.shape, v.dtype) for v in (rd, pt, lg, df, ag, smf, route)]
+        + [
+            pltpu.VMEM(pooled_shape, BF),
+            pltpu.SemaphoreType.DMA((len(arrays),)),
+            pltpu.SemaphoreType.DMA((PARTS,)),
+        ],
         compiler_params=pltpu.CompilerParams(vmem_limit_bytes=60 * 1024 * 1024),
         name="finish",
-    )(tab, rd, pt, lg, df, ag, smf, dpt, route)
+    )(tab, *arrays)
 
 
 def shards(pooled, widths, placement, route, labels, proj, senet_in, senet_out, bilinear, w_first, w_second, w_last):
     tab = lax.axis_index("tab").astype(jnp.int32).reshape(1)
-    fields = jnp.arange(FIELDS, dtype=jnp.int32)
-    inv = jnp.sum(jnp.where(placement[:, None] == fields[None, :], fields[:, None], 0), axis=0)
     rd, lg, df, ag, smf, dpt, pt = exchange(
-        inv, placement, widths, labels, jnp.swapaxes(proj, 1, 2), senet_in.T, senet_out, bilinear, w_first, w_second,
+        placement, widths, labels, jnp.swapaxes(proj, 1, 2), senet_in.T, senet_out, bilinear, w_first, w_second,
         w_last, pooled,
     )
     scores, dx, dproj, din, dout, dbil, dfirst, dsecond, dlast = finish(

time: 66.5 us -> 59.7 us (0.90)
  Pallas kernels: 64.4 us -> 58.8 us
  other arithmetic: 1.26 us -> 0 us
    pallas_call x2, Pallas kernels: 64.4 us -> 58.8 us  [the longest x1 55.2 us: exchange(): pl.pallas_call(main_kernel, in_specs=[smem] * 2 + [hbm] * len(arrays), ou...]
    reduce_sum x1 -> x0, other arithmetic: 1.26 us -> none  [shards(): jnp.sum(jnp.where(placement[:, None] == fields[None, :], fields[:, None],...]
where the time goes in v3:
time: 59.7 us; the launch traced here: 59.5 us
  Pallas kernels  58.8 us (98%)
  between operations  0.66 us (1%)
    pallas_call x1, Pallas kernels, exchange(): pl.pallas_call(main_kernel, in_specs=[smem] * 2 + [hbm] * len(arrays), ou...  55.2 us
    pallas_call x1, Pallas kernels, finish(): pl.pallas_call(finish_kernel, in_specs=[smem] + [hbm] * len(arrays), out_...  3.61 us

profile of v3, /device:TPU:0, one launch (start us, length us, event | category | flops | bytes accessed | tf_op | source)
XLA Modules:
  0.0 59.5 jit_solution(18142143626403854613)
XLA Ops:
  0.7 55.2 %exchange.1 = (bf16[64,32,128]{2,1,0:T(8,128)(2,1)}, f32[32,1,128]{2,1,0:T(1,128)}, f32[256,128]{1,0:T(8,128)}, bf16[32,16,128]{2,1,0:T(8,128)(2,1)}, f32[80,128...) custom-call(s32[64]{0:T(128)} %place_hbm.1, s32[64]{0:T(128)} %width_ref.1, s32[64]{0:T(128)} %place_hbm.1, ...), custom_call_target="tpu_custom_call" | custom-call | tf_op jit(solution)/shard_map/exchange/pallas_call | solution.py:531
  55.9 3.6 %finish.1 = (f32[1,128]{1,0:T(1,128)}, bf16[2,4096,128]{2,1,0:T(8,128)(2,1)}, f32[2,32,128]{2,1,0:T(8,128)}, f32[32,64]{1,0:T(8,128)}, f32[32,64]{1,0:T(8,128)},...) custom-call(s32[1]{0:T(128)} %bitcast.tab_ref, ...), custom_call_target="tpu_custom_call" | custom-call | tf_op jit(solution)/shard_map/finish/pallas_call | solution.py:650

commit v4 on v3

--- a/solution.py
+++ b/solution.py
@@ -64,9 +64,10 @@
 
 def main_kernel(
     place_ref, width_ref, place_hbm, labels_hbm, proj_hbm, sin_hbm, sout_hbm, bil_hbm, w1_hbm, w2_hbm, wl_hbm, pooled_hbm,
-    rd_ref, lg_ref, df_ref, ag_ref, smf_ref, dpt_ref, pt_ref,
+    dx_hbm, lg_ref, df_ref, ag_ref, smf_ref, dpt_ref,
+    rd_ref, pt_ref,
     place_vec, labels_ref, projs, sin_ref, sout_ref, bil_ref, w1, w2_ref, wl_ref, xs, e_ref, recv, emb, prod, du, sq, wts, dpw, dsq, js, jp, dpb, d2, d2p, demb, dslot, dfb, r1, r2, rz, sr, dz, d2b, rd1, rd2, rdz, inv_vec, inv_ref,
-    load_sem, es, er, ds, dr, ls, lr, gs, gr, ps, pr, s1, q1, s2, q2, sz, qz, ss, sq_r, sd, qd, s1d, q1d, s2d, q2d, szd, qzd,
+    load_sem, es, er, ds, dr, ls, lr, gs, gr, ps, pr, s1, q1, s2, q2, sz, qz, ss, sq_r, sd, qd, s1d, q1d, s2d, q2d, szd, qzd, out_sem,
 ):
     t = lax.axis_index("tab")
     r = lax.axis_index("rep")
@@ -90,13 +91,21 @@
     mate = {"tab": t + 1 - 2 * c}
     barrier = pltpu.get_barrier_semaphore()
 
-    def hello(i, _):
-        pl.semaphore_signal(barrier, inc=1, device_id={"tab": lax.rem(t + i, TAB)}, device_id_type=pl.DeviceIdType.MESH)
-        return 0
-
-    lax.fori_loop(1, TAB, hello, 0)
-    for d in range(1, REP):
+    def away(v):
+        return min(v, SIDE - v)
+
+    hops = sorted(
+        ((dx, dy, dc) for dx in range(SIDE) for dy in range(SIDE) for dc in range(2) if dx or dy or dc),
+        key=lambda h: -(away(h[0]) + away(h[1])),
+    )
+    others = [
+        (lax.rem(x + dx, SIDE) * SIDE + lax.rem(y + dy, SIDE)) * 2 + lax.rem(c + dc, 2) for dx, dy, dc in hops
+    ]
+
+    for d in (2, 1, 3):
         pl.semaphore_signal(barrier, inc=1, device_id={"rep": lax.rem(r + d, REP)}, device_id_type=pl.DeviceIdType.MESH)
+    for p in others:
+        pl.semaphore_signal(barrier, inc=1, device_id={"tab": p}, device_id_type=pl.DeviceIdType.MESH)
 
     pairs = (
         (proj_hbm, projs), (labels_hbm, labels_ref), (bil_hbm, bil_ref), (sin_hbm, sin_ref), (sout_hbm, sout_ref),
@@ -152,12 +161,8 @@
     def pair(p):
         return pl.ds(p * 2, 2)
 
-    def e_send(i, _):
-        p = lax.rem(t + i, TAB)
+    for p in others:
         send(e_ref.at[p], recv.at[pair(t)], es.at[p], er.at[t], {"tab": p})
-        return 0
-
-    lax.fori_loop(1, TAB, e_send, 0)
     recv[pair(t)] = e_ref[t]
 
     def e_wait(i, _):
@@ -242,12 +247,6 @@
     logit = jnp.sum(h2 * wl, axis=1, keepdims=True)
     lg_ref[t] = jnp.sum(jnp.where(square, logit, 0.0), axis=0, keepdims=True)
 
-    def l_send(i, _):
-        p = lax.rem(t + i, TAB)
-        send(lg_ref.at[t], lg_ref.at[t], ls.at[p], lr.at[t], {"tab": p})
-        return 0
-
-    lax.fori_loop(1, TAB, l_send, 0)
     grad = jax.nn.sigmoid(logit) - target
     d_last = jnp.sum(grad * h2, axis=0, keepdims=True)
     dp2 = (grad * wl * slope(pre_second)).astype(BF)
@@ -307,6 +306,8 @@
         send(dfb.at[i], r1.at[a], s1.at[d], q1.at[a], {"tab": at(i, b)})
     d_first_row(a)
 
+    for p in others:
+        send(lg_ref.at[t], lg_ref.at[t], ls.at[p], lr.at[t], {"tab": p})
     for d in range(1, SIDE):
         i = peer(a, d)
         got(rd1.at[i], s1d.at[d], q1d.at[i], {"tab": at(i, b)})
@@ -357,12 +358,8 @@
 
     lax.fori_loop(0, FIELDS, by_slot, 0, unroll=16)
 
-    def d_send(i, _):
-        p = lax.rem(t + i, TAB)
+    for p in others:
         send(dslot.at[pair(p)], rd_ref.at[pair(t)], ds.at[p], dr.at[t], {"tab": p})
-        return 0
-
-    lax.fori_loop(1, TAB, d_send, 0)
     rd_ref[pair(t)] = dslot[pair(t)]
 
     d_in = mm(d_act, squeeze, NT, HI)
@@ -384,13 +381,13 @@
         return r, [(lax.rem(r + d, REP), {"rep": lax.rem(r + d, REP)}) for d in range(1, REP)]
 
     def small_start(phase):
-        me, others = peers(phase)
-        for d, (_, dev) in enumerate(others):
+        me, rest = peers(phase)
+        for d, (_, dev) in enumerate(rest):
             send(sr.at[phase, me], sr.at[phase, me], ss.at[phase, d], sq_r.at[phase, me], dev)
 
     def small_end(phase):
-        me, others = peers(phase)
-        for d, (who, dev) in enumerate(others):
+        me, rest = peers(phase)
+        for d, (who, dev) in enumerate(rest):
             got(sr.at[phase, who], ss.at[phase, d], sq_r.at[phase, who], dev)
         size = 2 if phase == 0 else 4
         out = sr[phase, 0].astype(F32)
@@ -399,6 +396,37 @@
         return out
 
     small_start(0)
+
+    for d in range(1, SIDE):
+        i = lax.rem(a + d, SIDE)
+        got(r1.at[i], s1.at[d], q1.at[i], {"tab": at(i, b)})
+
+    def first_sum(k, _):
+        out = dfb[a, k].astype(F32)
+        for d in range(1, SIDE):
+            out = out + r1[lax.rem(a + d, SIDE), k].astype(F32)
+        dfb[a, k] = out.astype(BF)
+        return 0
+
+    for d in range(1, SIDE):
+        k = lax.rem(b + d, SIDE)
+        first_sum(k, 0)
+        send(dfb.at[a, k], r2.at[b], s2.at[d], q2.at[b], {"tab": at(a, k)})
+    first_sum(b, 0)
+
+    sr[1, a] = small_end(0).astype(BF)
+    small_start(1)
+
+    for d in range(1, SIDE):
+        k = lax.rem(b + d, SIDE)
+        got(r2.at[k], s2.at[d], q2.at[k], {"tab": at(a, k)})
+    out = dfb[a, b].astype(F32)
+    for d in range(1, SIDE):
+        out = out + r2[lax.rem(b + d, SIDE)].astype(F32)
+    rz[r] = out.astype(BF)
+    for d in range(1, REP):
+        o = lax.rem(r + d, REP)
+        send(rz.at[r], rz.at[r], sz.at[d], qz.at[r], {"rep": o})
 
     for d in range(1, REP):
         got(rdz.at[peer(r, d)], szd.at[d], qzd.at[peer(r, d)], {"rep": peer(r, d)})
@@ -408,32 +436,11 @@
     mine = block_of(t)
     ag_ref[mine] = out.astype(BF)
 
-    def g_send(i, _):
-        p = lax.rem(t + i, TAB)
+    for p in others:
         send(ag_ref.at[mine], ag_ref.at[mine], gs.at[p], gr.at[t], {"tab": p})
-        return 0
-
-    lax.fori_loop(1, TAB, g_send, 0)
-
-    for d in range(1, SIDE):
-        i = lax.rem(a + d, SIDE)
-        got(r1.at[i], s1.at[d], q1.at[i], {"tab": at(i, b)})
-
-    def first_sum(k, _):
-        out = dfb[a, k].astype(F32)
-        for d in range(1, SIDE):
-            out = out + r1[lax.rem(a + d, SIDE), k].astype(F32)
-        dfb[a, k] = out.astype(BF)
-        return 0
-
-    for d in range(1, SIDE):
-        k = lax.rem(b + d, SIDE)
-        first_sum(k, 0)
-        send(dfb.at[a, k], r2.at[b], s2.at[d], q2.at[b], {"tab": at(a, k)})
-    first_sum(b, 0)
-
-    sr[1, a] = small_end(0).astype(BF)
-    small_start(1)
+
+    sr[2, b] = small_end(1).astype(BF)
+    small_start(2)
 
 
     def d_wait(i, _):
@@ -454,19 +461,20 @@
         o = lax.rem(r + d, REP)
         send(dz.at[r], dz.at[r], sd.at[d], qd.at[r], {"rep": o})
 
-    sr[2, b] = small_end(1).astype(BF)
-    small_start(2)
-
-    for d in range(1, SIDE):
-        k = lax.rem(b + d, SIDE)
-        got(r2.at[k], s2.at[d], q2.at[k], {"tab": at(a, k)})
-    out = dfb[a, b].astype(F32)
-    for d in range(1, SIDE):
-        out = out + r2[lax.rem(b + d, SIDE)].astype(F32)
-    rz[r] = out.astype(BF)
-    for d in range(1, REP):
-        o = lax.rem(r + d, REP)
-        send(rz.at[r], rz.at[r], sz.at[d], qz.at[r], {"rep": o})
+    pt = pt_ref[...]
+    nil = jnp.zeros((E, LANES), BF)
+    wide = jnp.concatenate(
+        [jnp.concatenate([pt[:E], nil], axis=1), jnp.concatenate([nil, pt[E:]], axis=1)], axis=0
+    )
+    writes = []
+    for p in range(PARTS):
+        for k in range(p * (TAB // PARTS), (p + 1) * (TAB // PARTS)):
+            out = mm(rd_ref[2 * k : 2 * k + 2].reshape(2 * E, LANES), wide, TN).astype(BF)
+            xs[0, k * LANES : (k + 1) * LANES] = out[:, :LANES]
+            xs[1, k * LANES : (k + 1) * LANES] = out[:, LANES:]
+        piece = pl.ds(p * part, part)
+        writes.append(pltpu.make_async_copy(xs.at[:, piece], dx_hbm.at[:, piece], out_sem.at[p]))
+        writes[p].start()
 
     sr[3, r] = small_end(2).astype(BF)
     small_start(3)
@@ -515,9 +523,11 @@
         sent(d2b.at[a, k], s2d.at[d], q2d.at[k], {"tab": at(a, k)})
         sent(rdz.at[r], szd.at[d], qzd.at[r], {"rep": o})
         sent(dz.at[r], sd.at[d], qd.at[r], {"rep": o})
+    for copy in writes:
+        copy.wait()
     for phase in range(4):
-        me, others = peers(phase)
-        for d, (_, dev) in enumerate(others):
+        me, rest = peers(phase)
+        for d, (_, dev) in enumerate(rest):
             sent(sr.at[phase, me], ss.at[phase, d], sq_r.at[phase, me], dev)
 
 
@@ -531,17 +541,17 @@
     return pl.pallas_call(
         main_kernel,
         in_specs=[smem] * 2 + [hbm] * len(arrays),
-        out_specs=[vmem] * 7,
+        out_specs=[hbm] + [vmem] * 5,
         out_shape=[
-            jax.ShapeDtypeStruct((FIELDS, E, LANES), BF),
+            jax.ShapeDtypeStruct(pooled.shape, BF),
             jax.ShapeDtypeStruct((TAB, 1, LANES), F32),
             jax.ShapeDtypeStruct((BLOCK, LANES), F32),
             jax.ShapeDtypeStruct((TAB, 16, LANES), BF),
             jax.ShapeDtypeStruct((SMALL, LANES), F32),
             jax.ShapeDtypeStruct((2, E, LANES), F32),
-            jax.ShapeDtypeStruct((2 * E, LANES), BF),
         ],
-        scratch_shapes=[pltpu.VMEM(v.shape, v.dtype) for v in arrays]
+        scratch_shapes=[pltpu.VMEM((FIELDS, E, LANES), BF), pltpu.VMEM((2 * E, LANES), BF)]
+        + [pltpu.VMEM(v.shape, v.dtype) for v in arrays]
         + [
             pltpu.VMEM((TAB, 2, E, LANES), BF),
             pltpu.VMEM((FIELDS, E, LANES), BF),
@@ -577,7 +587,8 @@
         + [dma((3,))] * 2
         + [dma((4,))] * 6
         + [dma((4, 4))] * 2
-        + [dma((4,))] * 8,
+        + [dma((4,))] * 8
+        + [dma((PARTS,))],
         compiler_params=pltpu.CompilerParams(
             collective_id=0, has_side_effects=True, vmem_limit_bytes=60 * 1024 * 1024
         ),
@@ -586,37 +597,27 @@
 
 
 def finish_kernel(
-    tab_ref, rd_hbm, pt_hbm, lg_hbm, df_hbm, ag_hbm, smf_hbm, dpt_hbm, route_hbm,
+    tab_ref, ready_hbm, lg_hbm, df_hbm, ag_hbm, smf_hbm, dpt_hbm, route_hbm,
     scores_ref, dx_hbm, dproj_ref, din_ref, dout_ref, dbil_ref, dfirst_ref, dsecond_ref, dlast_ref,
-    rd_ref, pt_ref, lg_ref, df_ref, ag_ref, smf_ref, route_ref, dx, load_sem, out_sem,
+    lg_ref, df_ref, ag_ref, smf_ref, route_ref, dx, load_sem, out_sem,
 ):
     pairs = (
-        (rd_hbm, rd_ref), (pt_hbm, pt_ref), (lg_hbm, lg_ref), (route_hbm, route_ref), (smf_hbm, smf_ref),
-        (df_hbm, df_ref), (ag_hbm, ag_ref), (dpt_hbm, dproj_ref),
-    )
+        (lg_hbm, lg_ref), (route_hbm, route_ref), (smf_hbm, smf_ref), (df_hbm, df_ref), (ag_hbm, ag_ref),
+        (dpt_hbm, dproj_ref),
+    )
+    part = dx.shape[1] // PARTS
+    pieces = [pl.ds(p * part, part) for p in range(PARTS)]
+    reads = [pltpu.make_async_copy(ready_hbm.at[:, v], dx.at[:, v], load_sem.at[6 + p]) for p, v in enumerate(pieces)]
+    writes = [pltpu.make_async_copy(dx.at[:, v], dx_hbm.at[:, v], out_sem.at[p]) for p, v in enumerate(pieces)]
     loads = [pltpu.make_async_copy(src, dst, load_sem.at[i]) for i, (src, dst) in enumerate(pairs)]
-    for k in (1, 0, 2, 3, 4, 5, 6, 7):
-        loads[k].start()
-    loads[1].wait()
-    pt = pt_ref[...]
-    nil = jnp.zeros((E, LANES), BF)
-    wide = jnp.concatenate(
-        [jnp.concatenate([pt[:E], nil], axis=1), jnp.concatenate([nil, pt[E:]], axis=1)], axis=0
-    )
-    loads[0].wait()
-    part = dx.shape[1] // PARTS
-    writes = []
+    reads[0].start()
+    for copy in loads + reads[1:]:
+        copy.start()
     for p in range(PARTS):
-        for k in range(p * (TAB // PARTS), (p + 1) * (TAB // PARTS)):
-            out = mm(rd_ref[2 * k : 2 * k + 2].reshape(2 * E, LANES), wide, TN).astype(BF)
-            dx[0, k * LANES : (k + 1) * LANES] = out[:, :LANES]
-            dx[1, k * LANES : (k + 1) * LANES] = out[:, LANES:]
-        piece = pl.ds(p * part, part)
-        writes.append(pltpu.make_async_copy(dx.at[:, piece], dx_hbm.at[:, piece], out_sem.at[p]))
+        reads[p].wait()
         writes[p].start()
-
-    for k in range(2, len(pairs)):
-        loads[k].wait()
+    for copy in loads:
+        copy.wait()
     idx = route_ref[:, pl.ds(pl.multiple_of(tab_ref[0] * LANES, LANES), LANES)]
     table = lg_ref[...].reshape(TAB, LANES)
     low = jnp.broadcast_to(lax.rem(idx, LANES), (TAB, LANES))
@@ -638,11 +639,11 @@
         w.wait()
 
 
-def finish(tab, rd, pt, lg, df, ag, smf, dpt, route, pooled_shape):
+def finish(tab, ready, lg, df, ag, smf, dpt, route, pooled_shape):
     vmem = pl.BlockSpec(memory_space=pltpu.VMEM)
     smem = pl.BlockSpec(memory_space=pltpu.SMEM)
     hbm = pl.BlockSpec(memory_space=pltpu.HBM)
-    arrays = (rd, pt, lg, df, ag, smf, dpt, route)
+    arrays = (ready, lg, df, ag, smf, dpt, route)
     outs = [
         ((1, LANES), F32), (pooled_shape, BF), ((2, E, LANES), F32), ((E, FIELDS), F32), ((E, FIELDS), F32),
         ((E, E), F32), ((LANES, HID), F32), ((HID, HID), F32), ((1, HID), F32),
@@ -652,10 +653,10 @@
         in_specs=[smem] + [hbm] * len(arrays),
         out_specs=[vmem, hbm] + [vmem] * 7,
         out_shape=[jax.ShapeDtypeStruct(s, d) for s, d in outs],
-        scratch_shapes=[pltpu.VMEM(v.shape, v.dtype) for v in (rd, pt, lg, df, ag, smf, route)]
+        scratch_shapes=[pltpu.VMEM(v.shape, v.dtype) for v in (lg, df, ag, smf, route)]
         + [
             pltpu.VMEM(pooled_shape, BF),
-            pltpu.SemaphoreType.DMA((len(arrays),)),
+            pltpu.SemaphoreType.DMA((6 + PARTS,)),
             pltpu.SemaphoreType.DMA((PARTS,)),
         ],
         compiler_params=pltpu.CompilerParams(vmem_limit_bytes=60 * 1024 * 1024),
@@ -665,12 +666,12 @@
 
 def shards(pooled, widths, placement, route, labels, proj, senet_in, senet_out, bilinear, w_first, w_second, w_last):
     tab = lax.axis_index("tab").astype(jnp.int32).reshape(1)
-    rd, lg, df, ag, smf, dpt, pt = exchange(
+    ready, lg, df, ag, smf, dpt = exchange(
         placement, widths, labels, jnp.swapaxes(proj, 1, 2), senet_in.T, senet_out, bilinear, w_first, w_second,
         w_last, pooled,
     )
     scores, dx, dproj, din, dout, dbil, dfirst, dsecond, dlast = finish(
-        tab, rd, pt, lg, df, ag, smf, dpt, route, pooled.shape
+        tab, ready, lg, df, ag, smf, dpt, route, pooled.shape
     )
     return scores, dx, jnp.swapaxes(dproj, 1, 2), din.T, dout, dbil, dfirst, dsecond, dlast[0]
 

time: 59.7 us -> 56.4 us (0.945)
  Pallas kernels: 58.8 us -> 55.6 us
    pallas_call x1, Pallas kernels: 55.2 us -> 52.2 us  [exchange(): pl.pallas_call(main_kernel, in_specs=[smem] * 2 + [hbm] * len(arrays), ou...]
where the time goes in v4:
time: 56.4 us; the launch traced here: 56.2 us
  Pallas kernels  55.6 us (99%)
  between operations  0.66 us (1%)
    pallas_call x1, Pallas kernels, exchange(): pl.pallas_call(main_kernel, in_specs=[smem] * 2 + [hbm] * len(arrays), ou...  52.2 us
    pallas_call x1, Pallas kernels, finish(): pl.pallas_call(finish_kernel, in_specs=[smem] + [hbm] * len(arrays), out_...  3.39 us

profile of v4, /device:TPU:0, one launch (start us, length us, event | category | flops | bytes accessed | tf_op | source)
XLA Modules:
  0.0 56.2 jit_solution(9102999392513496734)
XLA Ops:
  0.7 52.2 %exchange.1 = (bf16[2,4096,128]{2,1,0:T(8,128)(2,1)}, f32[32,1,128]{2,1,0:T(1,128)}, f32[256,128]{1,0:T(8,128)}, bf16[32,16,128]{2,1,0:T(8,128)(2,1)}, f32[80,128]{1,0:T(8,128)}, /*index=5*/f32[2,32,128]{2,1,0:T(8,128)}) custom-call(s32[64]{0:T(128)} %place_hbm.1, s32[64]{0:T(128)} %width_ref.1, s32[64]{0:T(128)} %place_hbm.1, s32[1,4096]{1,0:T(1,128)} %labels_hbm.1, ...), custom_call_target="tpu_custom_call" | custom-call | tf_op jit(solution)/shard_map/exchange/pallas_call | solution.py:541
  52.8 3.4 %finish.1 = (f32[1,128]{1,0:T(1,128)}, bf16[2,4096,128]{2,1,0:T(8,128)(2,1)}, f32[2,32,128]{2,1,0:T(8,128)}, f32[32,64]{1,0:T(8,128)}, f32[32,64]{1,0:T(8,128)},...) custom-call(s32[1]{0:T(128)} %bitcast.tab_ref, ...), custom_call_target="tpu_custom_call" | custom-call | tf_op jit(solution)/shard_map/finish/pallas_call | solution.py:651

commit v5 on v4

--- a/solution.py
+++ b/solution.py
@@ -375,10 +375,10 @@
         if phase == 0:
             return c, [(1 - c, mate)]
         if phase == 1:
+            return r, [(lax.rem(r + d, REP), {"rep": lax.rem(r + d, REP)}) for d in range(1, REP)]
+        if phase == 2:
             return a, [(lax.rem(a + d, SIDE), {"tab": at(lax.rem(a + d, SIDE), b)}) for d in range(1, SIDE)]
-        if phase == 2:
-            return b, [(lax.rem(b + d, SIDE), {"tab": at(a, lax.rem(b + d, SIDE))}) for d in range(1, SIDE)]
-        return r, [(lax.rem(r + d, REP), {"rep": lax.rem(r + d, REP)}) for d in range(1, REP)]
+        return b, [(lax.rem(b + d, SIDE), {"tab": at(a, lax.rem(b + d, SIDE))}) for d in range(1, SIDE)]
 
     def small_start(phase):
         me, rest = peers(phase)
@@ -396,6 +396,9 @@
         return out
 
     small_start(0)
+    sr[1, r] = small_end(0).astype(BF)
+    small_start(1)
+
 
     for d in range(1, SIDE):
         i = lax.rem(a + d, SIDE)
@@ -414,8 +417,9 @@
         send(dfb.at[a, k], r2.at[b], s2.at[d], q2.at[b], {"tab": at(a, k)})
     first_sum(b, 0)
 
-    sr[1, a] = small_end(0).astype(BF)
-    small_start(1)
+
+    sr[2, a] = small_end(1).astype(BF)
+    small_start(2)
 
     for d in range(1, SIDE):
         k = lax.rem(b + d, SIDE)
@@ -439,9 +443,6 @@
     for p in others:
         send(ag_ref.at[mine], ag_ref.at[mine], gs.at[p], gr.at[t], {"tab": p})
 
-    sr[2, b] = small_end(1).astype(BF)
-    small_start(2)
-
 
     def d_wait(i, _):
         p = lax.rem(t + i, TAB)
@@ -449,6 +450,9 @@
         return 0
 
     lax.fori_loop(1, TAB, d_wait, 0)
+
+    sr[3, b] = small_end(2).astype(BF)
+    small_start(3)
 
     def proj_pass(j, acc):
         left = jnp.concatenate([rd_ref[pair(2 * j)].reshape(2 * E, LANES), rd_ref[pair(2 * j + 1)].reshape(2 * E, LANES)], axis=1)
@@ -476,8 +480,6 @@
         writes.append(pltpu.make_async_copy(xs.at[:, piece], dx_hbm.at[:, piece], out_sem.at[p]))
         writes[p].start()
 
-    sr[3, r] = small_end(2).astype(BF)
-    small_start(3)
 
     for d in range(1, REP):
         o = lax.rem(r + d, REP)

time: 56.4 us -> 53.2 us (0.943)
  Pallas kernels: 55.6 us -> 52.4 us
    pallas_call x1, Pallas kernels: 52.2 us -> 49 us  [exchange(): pl.pallas_call(main_kernel, in_specs=[smem] * 2 + [hbm] * len(arrays), ou...]
where the time goes in v5:
time: 53.2 us; the launch traced here: 53 us
  Pallas kernels  52.4 us (98%)
  between operations  0.66 us (1%)
    pallas_call x1, Pallas kernels, exchange(): pl.pallas_call(main_kernel, in_specs=[smem] * 2 + [hbm] * len(arrays), ou...  49 us
    pallas_call x1, Pallas kernels, finish(): pl.pallas_call(finish_kernel, in_specs=[smem] + [hbm] * len(arrays), out_...  3.39 us

profile of v5, /device:TPU:0, one launch (start us, length us, event | category | flops | bytes accessed | tf_op | source)
XLA Modules:
  0.0 53.0 jit_solution(17595035805779389006)
XLA Ops:
  0.7 49.0 %exchange.1 = (bf16[2,4096,128]{2,1,0:T(8,128)(2,1)}, f32[32,1,128]{2,1,0:T(1,128)}, f32[256,128]{1,0:T(8,128)}, bf16[32,16,128]{2,1,0:T(8,128)(2,1)}, f32[80,128]{1,0:T(8,128)}, /*index=5*/f32[2,32,128]{2,1,0:T(8,128)}) custom-call(s32[64]{0:T(128)} %place_hbm.1, s32[64]{0:T(128)} %width_ref.1, s32[64]{0:T(128)} %place_hbm.1, s32[1,4096]{1,0:T(1,128)} %labels_hbm.1, ...), custom_call_target="tpu_custom_call" | custom-call | tf_op jit(solution)/shard_map/exchange/pallas_call | solution.py:543
  49.6 3.4 %finish.1 = (f32[1,128]{1,0:T(1,128)}, bf16[2,4096,128]{2,1,0:T(8,128)(2,1)}, f32[2,32,128]{2,1,0:T(8,128)}, f32[32,64]{1,0:T(8,128)}, f32[32,64]{1,0:T(8,128)},...) custom-call(s32[1]{0:T(128)} %bitcast.tab_ref, ...), custom_call_target="tpu_custom_call" | custom-call | tf_op jit(solution)/shard_map/finish/pallas_call | solution.py:653

commit v6 on v5

--- a/solution.py
+++ b/solution.py
@@ -18,7 +18,7 @@
 E = 32
 TAB = 32
 REP = 4
-EARLY = 4
+EARLY = 2
 SIDE = 4
 PARTS = 4
 LANES = 128
@@ -275,7 +275,7 @@
             out.append(sums[k] + jnp.sum(dq, axis=0))
         return (*out, bil_sum)
 
-    sums = lax.fori_loop(0, EARLY, fourth_pass, (zero, zero, jnp.zeros((E, E), F32)), unroll=4)
+    sums = lax.fori_loop(0, EARLY, fourth_pass, (zero, zero, jnp.zeros((E, E), F32)), unroll=2)
 
     def peer(me, d):
         return lax.rem(me + d, SIDE)
@@ -297,13 +297,16 @@
         )
         out = mm(left, both, NN).astype(BF)
         for k in range(SIDE):
-            dfb[i, k, 0:LANES] = out[k * LANES : (k + 1) * LANES, :LANES]
-            dfb[i, k, LANES:] = out[k * LANES : (k + 1) * LANES, LANES:]
+            for h in range(2):
+                dfb[h, i, k] = out[k * LANES : (k + 1) * LANES, h * LANES : (h + 1) * LANES]
 
     for d in range(1, SIDE):
         i = peer(a, d)
         d_first_row(i)
-        send(dfb.at[i], r1.at[a], s1.at[d], q1.at[a], {"tab": at(i, b)})
+        send(dfb.at[0, i], r1.at[0, a], s1.at[0, d], q1.at[0, a], {"tab": at(i, b)})
+    for d in range(1, SIDE):
+        i = peer(a, d)
+        send(dfb.at[1, i], r1.at[1, a], s1.at[1, d], q1.at[1, a], {"tab": at(i, b)})
     d_first_row(a)
 
     for p in others:
@@ -319,7 +322,7 @@
         k = peer(b, d)
         send(d2b.at[a, k], rd2.at[b], s2d.at[d], q2d.at[b], {"tab": at(a, k)})
 
-    sum_q, sum_qs, d_bil = lax.fori_loop(EARLY, groups, fourth_pass, sums, unroll=4)
+    sum_q, sum_qs, d_bil = lax.fori_loop(EARLY, groups, fourth_pass, sums, unroll=6)
 
     for d in range(1, SIDE):
         k = peer(b, d)
@@ -400,37 +403,35 @@
     small_start(1)
 
 
-    for d in range(1, SIDE):
-        i = lax.rem(a + d, SIDE)
-        got(r1.at[i], s1.at[d], q1.at[i], {"tab": at(i, b)})
-
-    def first_sum(k, _):
-        out = dfb[a, k].astype(F32)
+    def first_sum(h, k):
+        out = dfb[h, a, k].astype(F32)
         for d in range(1, SIDE):
-            out = out + r1[lax.rem(a + d, SIDE), k].astype(F32)
-        dfb[a, k] = out.astype(BF)
-        return 0
-
-    for d in range(1, SIDE):
-        k = lax.rem(b + d, SIDE)
-        first_sum(k, 0)
-        send(dfb.at[a, k], r2.at[b], s2.at[d], q2.at[b], {"tab": at(a, k)})
-    first_sum(b, 0)
-
+            out = out + r1[h, peer(a, d), k].astype(F32)
+        dfb[h, a, k] = out.astype(BF)
+
+    for h in range(2):
+        for d in range(1, SIDE):
+            i = peer(a, d)
+            got(r1.at[h, i], s1.at[h, d], q1.at[h, i], {"tab": at(i, b)})
+        for d in range(1, SIDE):
+            k = peer(b, d)
+            first_sum(h, k)
+            send(dfb.at[h, a, k], r2.at[h, b], s2.at[h, d], q2.at[h, b], {"tab": at(a, k)})
+        first_sum(h, b)
 
     sr[2, a] = small_end(1).astype(BF)
     small_start(2)
 
-    for d in range(1, SIDE):
-        k = lax.rem(b + d, SIDE)
-        got(r2.at[k], s2.at[d], q2.at[k], {"tab": at(a, k)})
-    out = dfb[a, b].astype(F32)
-    for d in range(1, SIDE):
-        out = out + r2[lax.rem(b + d, SIDE)].astype(F32)
-    rz[r] = out.astype(BF)
-    for d in range(1, REP):
-        o = lax.rem(r + d, REP)
-        send(rz.at[r], rz.at[r], sz.at[d], qz.at[r], {"rep": o})
+    for h in range(2):
+        for d in range(1, SIDE):
+            k = peer(b, d)
+            got(r2.at[h, k], s2.at[h, d], q2.at[h, k], {"tab": at(a, k)})
+        out = dfb[h, a, b].astype(F32)
+        for d in range(1, SIDE):
+            out = out + r2[h, peer(b, d)].astype(F32)
+        rz[h, r] = out.astype(BF)
+        for d in range(1, REP):
+            send(rz.at[h, r], rz.at[h, r], sz.at[h, d], qz.at[h, r], {"rep": peer(r, d)})
 
     for d in range(1, REP):
         got(rdz.at[peer(r, d)], szd.at[d], qzd.at[peer(r, d)], {"rep": peer(r, d)})
@@ -481,13 +482,14 @@
         writes[p].start()
 
 
-    for d in range(1, REP):
-        o = lax.rem(r + d, REP)
-        got(rz.at[o], sz.at[d], qz.at[o], {"rep": o})
-    out = rz[0].astype(F32)
-    for k in range(1, REP):
-        out = out + rz[k].astype(F32)
-    df_ref[...] = out
+    for h in range(2):
+        for d in range(1, REP):
+            o = peer(r, d)
+            got(rz.at[h, o], sz.at[h, d], qz.at[h, o], {"rep": o})
+        out = rz[h, 0].astype(F32)
+        for k in range(1, REP):
+            out = out + rz[h, k].astype(F32)
+        df_ref[h * LANES : (h + 1) * LANES] = out
 
     for d in range(1, REP):
         o = lax.rem(r + d, REP)
@@ -518,9 +520,10 @@
         i = lax.rem(a + d, SIDE)
         k = lax.rem(b + d, SIDE)
         o = lax.rem(r + d, REP)
-        sent(dfb.at[i], s1.at[d], q1.at[i], {"tab": at(i, b)})
-        sent(dfb.at[a, k], s2.at[d], q2.at[k], {"tab": at(a, k)})
-        sent(rz.at[r], sz.at[d], qz.at[r], {"rep": o})
+        for h in range(2):
+            sent(dfb.at[h, i], s1.at[h, d], q1.at[h, i], {"tab": at(i, b)})
+            sent(dfb.at[h, a, k], s2.at[h, d], q2.at[h, k], {"tab": at(a, k)})
+            sent(rz.at[h, r], sz.at[h, d], qz.at[h, r], {"rep": o})
         sent(d2b.at[i], s1d.at[d], q1d.at[i], {"tab": at(i, b)})
         sent(d2b.at[a, k], s2d.at[d], q2d.at[k], {"tab": at(a, k)})
         sent(rdz.at[r], szd.at[d], qzd.at[r], {"rep": o})
@@ -571,10 +574,10 @@
             pltpu.VMEM((16, 16, LANES), BF),
             pltpu.VMEM((FIELDS, E, LANES), BF),
             pltpu.VMEM((FIELDS, E, LANES), BF),
-            pltpu.VMEM((SIDE, SIDE, BLOCK, LANES), BF),
-            pltpu.VMEM((SIDE, SIDE, BLOCK, LANES), BF),
-            pltpu.VMEM((SIDE, BLOCK, LANES), BF),
-            pltpu.VMEM((REP, BLOCK, LANES), BF),
+            pltpu.VMEM((2, SIDE, SIDE, LANES, LANES), BF),
+            pltpu.VMEM((2, SIDE, SIDE, LANES, LANES), BF),
+            pltpu.VMEM((2, SIDE, LANES, LANES), BF),
+            pltpu.VMEM((2, REP, LANES, LANES), BF),
             pltpu.VMEM((4, 4, SMALL, LANES), BF),
             pltpu.VMEM((REP, 2 * E, LANES), BF),
             pltpu.VMEM((SIDE, SIDE, 16, LANES), BF),
@@ -587,7 +590,7 @@
         ]
         + [dma((TAB,))] * 8
         + [dma((3,))] * 2
-        + [dma((4,))] * 6
+        + [dma((2, 4))] * 6
         + [dma((4, 4))] * 2
         + [dma((4,))] * 8
         + [dma((PARTS,))],

time: 53.2 us -> 52.8 us (level)
  no operation moved by 1% of the time
where the time goes in v6:
time: 52.8 us; the launch traced here: 52.6 us
  Pallas kernels  52 us (98%)
  between operations  0.66 us (1%)
    pallas_call x1, Pallas kernels, exchange(): pl.pallas_call(main_kernel, in_specs=[smem] * 2 + [hbm] * len(arrays), ou...  48.6 us
    pallas_call x1, Pallas kernels, finish(): pl.pallas_call(finish_kernel, in_specs=[smem] + [hbm] * len(arrays), out_...  3.39 us

profile of v6, /device:TPU:0, one launch (start us, length us, event | category | flops | bytes accessed | tf_op | source)
XLA Modules:
  0.0 52.6 jit_solution(13690129103029063748)
XLA Ops:
  0.7 48.6 %exchange.1 = (bf16[2,4096,128]{2,1,0:T(8,128)(2,1)}, f32[32,1,128]{2,1,0:T(1,128)}, f32[256,128]{1,0:T(8,128)}, bf16[32,16,128]{2,1,0:T(8,128)(2,1)}, f32[80,128]{1,0:T(8,128)}, /*index=5*/f32[2,32,128]{2,1,0:T(8,128)}) custom-call(s32[64]{0:T(128)} %place_hbm.1, s32[64]{0:T(128)} %width_ref.1, s32[64]{0:T(128)} %place_hbm.1, s32[1,4096]{1,0:T(1,128)} %labels_hbm.1, ...), custom_call_target="tpu_custom_call" | custom-call | tf_op jit(solution)/shard_map/exchange/pallas_call | solution.py:546
  49.3 3.4 %finish.1 = (f32[1,128]{1,0:T(1,128)}, bf16[2,4096,128]{2,1,0:T(8,128)(2,1)}, f32[2,32,128]{2,1,0:T(8,128)}, f32[32,64]{1,0:T(8,128)}, f32[32,64]{1,0:T(8,128)},...) custom-call(s32[1]{0:T(128)} %bitcast.tab_ref, ...), custom_call_target="tpu_custom_call" | custom-call | tf_op jit(solution)/shard_map/finish/pallas_call | solution.py:656
